TPU v7x, 256 devices: a whole 4x4x8 slice. The times are simulated.
256 devices in a mesh: circ: 64 (over z, y, core), ax: 4 (over x).
Axes of the slice: x: 4, y: 4, z: 8, core: 2. Of those that a mesh axis runs over, the one named last changes fastest.
Arguments:
- adjoint: float32 [5, 2048, 16, 512], P(None, 'circ', 'ax'), may hold values from -6 to 6
- source: float32 [5, 2048, 16, 512], P(None, 'circ', 'ax'), may hold values from -6 to 6
- step_size: float32 [2048, 16, 512], P('circ', 'ax'), may hold values from 0.3 to 3
- lengths: int32 [2048, 16], P('circ', 'ax'), may hold values from 128 to 512, as said below
- line_owner: int32 [4, 2048, 4, 1], P('ax', 'circ'), may hold values from 0 to 63; in each aligned block of 128 rows (0 to 127, 128 to 255, ..., all dimensions but the last counted through in order) at most 4 rows name the same one
- coupling: float32 [4, 5, 5], replicated, may hold values from -1.25 to 1.25
- lower_coef: bfloat16 [4, 16384, 5, 512], P('ax', 'circ'), may hold values from 0.5 to 0.99609375
- upper_coef: bfloat16 [4, 16384, 5, 512], P('ax', 'circ'), may hold values from 0.5 to 0.99609375
- pivot_inverse: bfloat16 [4, 16384, 25, 512], P('ax', 'circ'), may hold values from -0.1796875 to 0.1796875
Outputs:
- updated: float32 [5, 2048, 16, 512], P(None, 'circ', 'ax')
Inputs may be any that keep to these rules, and one draw needn't show every extreme that they name: `lengths`: on every device some column has the full 512 points. `line_owner`: among the lines of one device at most 4 name the same owner, and this bound is reached.
All inputs are finite; a program needn't handle non-finite values.
Results may differ from a plain program's by a relative error of at most 0.0003.
Values may be sent and summed in bfloat16 or wider, within the bound.
A program may use at most 128 MiB of HBM per device.

v0:
```python
import functools

import jax
import jax.numpy as jnp
from jax import lax
from jax.experimental import pallas as pl
from jax.experimental.pallas import tpu as pltpu
from jax.sharding import PartitionSpec as P


def extended(block, sides, width, periodic):
    for axis, dim in sides:
        count = lax.axis_size(axis)
        forward = [(i, i + 1) for i in range(count - 1)]
        if periodic:
            forward.append((count - 1, 0))
        backward = [(target, source) for source, target in forward]
        low = lax.ppermute(
            lax.slice_in_dim(block, block.shape[dim] - width, None, axis=dim), axis, forward
        )
        high = lax.ppermute(lax.slice_in_dim(block, 0, width, axis=dim), axis, backward)
        block = jnp.concatenate([low, block, high], axis=dim)
    return block


def scan_forward(coef, value, pos):
    points = value.shape[-1]
    shift = 1
    while shift < points:
        keep = pos >= shift
        value = value + coef * jnp.where(keep, pltpu.roll(value, shift, 2), 0.0)
        coef = coef * pltpu.roll(coef, shift, 2)
        shift *= 2
    return value


def scan_backward(coef, value, pos):
    points = value.shape[-1]
    shift = 1
    while shift < points:
        keep = pos < points - shift
        value = value + coef * jnp.where(keep, pltpu.roll(value, points - shift, 2), 0.0)
        coef = coef * pltpu.roll(coef, points - shift, 2)
        shift *= 2
    return value


def solve_kernel(rhs_ref, lens_ref, lower_ref, upper_ref, pivot_ref, adj_ref, out_ref):
    fields, rows, points = rhs_ref.shape
    pos = lax.broadcasted_iota(jnp.int32, (fields, rows, points), 2)
    active = pos < lens_ref[...][None, :, :]
    forward_coef = jnp.where(active, -lower_ref[...].astype(jnp.float32), 0.0)
    interim = scan_forward(forward_coef, jnp.where(active, rhs_ref[...], 0.0), pos)
    applied = []
    for f in range(fields):
        total = pivot_ref[f * fields].astype(jnp.float32) * interim[0]
        for g in range(1, fields):
            total = total + pivot_ref[f * fields + g].astype(jnp.float32) * interim[g]
        applied.append(total)
    applied = jnp.stack(applied, axis=0)
    backward_coef = jnp.where(active, -upper_ref[...].astype(jnp.float32), 0.0)
    solved = scan_backward(backward_coef, jnp.where(active, applied, 0.0), pos)
    out_ref[...] = adj_ref[...] + solved


def line_solve(rhs, lens, lower, upper, pivot, adj, block_rows=16):
    fields, lines, points = rhs.shape
    blocks = pivot.shape[0]
    grid = (lines // block_rows,)
    field_spec = pl.BlockSpec((fields, block_rows, points), lambda i: (0, i, 0))
    return pl.pallas_call(
        solve_kernel,
        out_shape=jax.ShapeDtypeStruct(rhs.shape, jnp.float32),
        grid=grid,
        in_specs=[
            field_spec,
            pl.BlockSpec((block_rows, 1), lambda i: (i, 0)),
            field_spec,
            field_spec,
            pl.BlockSpec((blocks, block_rows, points), lambda i: (0, i, 0)),
            field_spec,
        ],
        out_specs=field_spec,
    )(rhs, lens, lower, upper, pivot, adj)


def per_device(
    adjoint, source, step_size, lengths, line_owner, coupling, lower_coef, upper_coef, pivot_inverse
):
    fields, circ_cells, axial_cells, points = adjoint.shape
    line_count = circ_cells * axial_cells
    circ_devices = lax.axis_size("circ")
    capacity = 2 * line_count // circ_devices
    circ_padded = extended(adjoint, (("circ", 1),), 1, True)
    axial_padded = extended(adjoint, (("ax", 2),), 1, False)
    neighbours = (
        circ_padded[:, 2:],
        circ_padded[:, :-2],
        axial_padded[:, :, 2:],
        axial_padded[:, :, :-2],
    )
    coupled = None
    for k, near in enumerate(neighbours):
        for g in range(fields):
            term = coupling[k, :, g][:, None, None, None] * near[g][None]
            coupled = term if coupled is None else coupled + term
    residual = source - adjoint + step_size[None] * coupled
    line_rhs = residual.reshape(fields, line_count, points)
    line_adj = adjoint.reshape(fields, line_count, points)
    line_lens = lengths.reshape(line_count, 1)
    targets = line_owner.reshape(line_count)
    ordinal = jnp.arange(line_count)
    earlier_same = (targets[:, None] == targets[None, :]) & (ordinal[None, :] < ordinal[:, None])
    slot_ids = targets * capacity + jnp.sum(earlier_same, axis=1)
    lower_here, upper_here, pivot_here = (
        lax.all_to_all(lower_coef[0], "circ", split_axis=0, concat_axis=0, tiled=True),
        lax.all_to_all(upper_coef[0], "circ", split_axis=0, concat_axis=0, tiled=True),
        lax.all_to_all(pivot_inverse[0], "circ", split_axis=0, concat_axis=0, tiled=True),
    )
    lower_rows = jnp.take(lower_here, slot_ids, axis=0).transpose(1, 0, 2)
    upper_rows = jnp.take(upper_here, slot_ids, axis=0).transpose(1, 0, 2)
    pivot_rows = jnp.take(pivot_here, slot_ids, axis=0).transpose(1, 0, 2)
    updated = line_solve(line_rhs, line_lens, lower_rows, upper_rows, pivot_rows, line_adj)
    return updated.reshape(fields, circ_cells, axial_cells, points)


def solution(mesh):
    placed = (
        P(None, "circ", "ax", None),
        P(None, "circ", "ax", None),
        P("circ", "ax", None),
        P("circ", "ax"),
        P("ax", "circ", None, None),
        P(),
        P("ax", "circ", None, None),
        P("ax", "circ", None, None),
        P("ax", "circ", None, None),
    )
    return jax.shard_map(
        per_device,
        mesh=mesh,
        in_specs=placed,
        out_specs=P(None, "circ", "ax", None),
        check_vma=False,
    )
```

profile of v0, /device:TPU:25, one launch (start us, length us, event | category | flops | bytes accessed | tf_op | source)
XLA Modules:
  0.0 362.6 jit_solution(705131006960471162)
XLA Ops:
  0.0 3.4 copy.68
  3.4 12.3 %all-to-all-start = ((bf16[256,5,512]{2,1,0:T(8,128)(2,1)}), bf16[256,5,512]{2,1,0:T(8,128)(2,1)S(1)}, u32[]{:S(2)}, u32[]{:S(2)}) async-start(bf16[256,5,512]{2,1,0:T(8,128)(2,1)} %bitcast.68), calls=%async_computation | async-start | bytes 4194304 | tf_op jit(solution)/shard_map/all_to_all | solution.py:116
  15.7 2.1 copy.67
  17.9 47.5 %all-to-all-done = bf16[256,5,512]{2,1,0:T(8,128)(2,1)S(1)} async-done(((bf16[256,5,512]{2,1,0:T(8,128)(2,1)}), bf16[256,5,512]{2,1,0:T(8,128)(2,1)S(1)}, u32[]{:S(2)}, u32[]{:S(2)}) %all-to-all-start) | async-done | bytes 1310752 | tf_op jit(solution)/shard_map/all_to_all | solution.py:116
  65.4 1.3 copy-done.1
  66.7 7.2 %all-to-all-start.1 = ((bf16[256,5,512]{2,1,0:T(8,128)(2,1)}), bf16[256,5,512]{2,1,0:T(8,128)(2,1)}, u32[]{:S(2)}, u32[]{:S(2)}) async-start(bf16[256,5,512]{2,1,0:T(8,128)(2,1)} %bitcast.67), calls=%async_computation.1 | async-start | bytes 4194304 | tf_op jit(solution)/shard_map/all_to_all | solution.py:117
  73.9 10.0 %copy.66 = bf16[1,256,25,512]{3,2,1,0:T(8,128)(2,1)} copy(bf16[1,256,25,512]{3,1,2,0:T(8,128)(2,1)} %param.19) | data formatting | bytes 13107200 | tf_op args[8]
  84.0 39.5 %all-to-all-done.1 = bf16[256,5,512]{2,1,0:T(8,128)(2,1)} async-done(((bf16[256,5,512]{2,1,0:T(8,128)(2,1)}), bf16[256,5,512]{2,1,0:T(8,128)(2,1)}, u32[]{:S(2)}, u32[]{:S(2)}) %all-to-all-start.1) | async-done | bytes 1310752 | tf_op jit(solution)/shard_map/all_to_all | solution.py:117
  123.5 7.4 %all-to-all-start.2 = ((bf16[256,25,512]{2,1,0:T(8,128)(2,1)}), bf16[256,25,512]{2,1,0:T(8,128)(2,1)}, u32[]{:S(2)}, u32[]{:S(2)}) async-start(bf16[256,25,512]{2,1,0:T(8,128)(2,1)} %bitcast.69), calls=%async_computation.2 | async-start | bytes 16777216 | tf_op jit(solution)/shard_map/all_to_all | solution.py:118
  131.0 1.5 collective-permute-start.1
  132.5 0.5 fusion.8
  133.0 1.3 collective-permute-start.2
  134.4 4.2 %collective-permute-start.3 = (f32[5,32,1,512]{3,1,2,0:T(8,128)S(1)}, f32[5,32,1,512]{3,1,2,0:T(8,128)S(1)}, u32[]{:S(2)}, u32[]{:S(2)}) collective-permute-start(f32[5,32,1,512]{3,1,2,0:T(8,128)S(1)} %copy.53), channel_id=1, source_target_pairs={{0,1},{1,2},{2,3},{4,5},{5,6},{6,7},{8,9},{9,10},{10,11},{12,13},{... | collective-permute-start | bytes 983048 | tf_op jit(solution)/shard_map/ppermute | solution.py:18
  138.6 0.1 copy.43
  138.7 0.1 reshape.80
  138.8 0.1 copy.49
  138.9 0.1 mul.476
  139.0 0.2 convert_reduce_fusion
  139.2 0.2 slice_reduce_fusion.1
  139.4 0.4 slice_reduce_fusion.19
  139.8 0.0 copy-start.7
  139.8 1.5 reshape.81.adj_ref
  141.3 0.1 copy.42
  141.4 0.7 reshape.113.lens_ref
  142.1 166.7 %collective-permute-done.1 = f32[5,1,4,512]{3,2,1,0:T(4,128)S(1)} collective-permute-done((f32[5,1,4,512]{3,2,1,0:T(4,128)S(1)}, f32[5,1,4,512]{3,2,1,0:T(4,128)S(1)}, u32[]{:S(2)}, u32[]{:S(2)}) %collective-permute-start.1) | collective-permute-done | bytes 40992 | tf_op jit(solution)/shard_map/ppermute | solution.py:18
  308.8 0.5 constant_dynamic-update-slice_fusion.1
  309.3 5.1 %collective-permute-done = f32[5,1,4,512]{3,2,1,0:T(4,128)S(1)} collective-permute-done((f32[5,1,4,512]{3,2,1,0:T(4,128)S(1)}, f32[5,1,4,512]{3,2,1,0:T(4,128)S(1)}, u32[]{:S(2)}, u32[]{:S(2)}) %collective-permute-start) | collective-permute-done | bytes 40992 | tf_op jit(solution)/shard_map/ppermute | solution.py:21
  314.5 0.2 slice_bitcast_fusion.9
  314.7 0.2 slice_bitcast_fusion.4
  315.0 0.0 collective-permute-done.2
  315.0 0.3 copy.39
  315.3 0.0 collective-permute-done.3
  315.3 0.3 copy.41
  315.7 0.8 maximum_bitcast_fusion.7
  316.4 0.0 copy-start.2
  316.4 0.0 copy-start.4
  316.5 0.6 maximum_bitcast_fusion.3
  317.1 0.7 copy-done.2
  317.8 0.0 copy-done.4
  317.8 4.7 %multiply_add_fusion = f32[5,32,4,512]{3,2,1,0:T(4,128)S(1)} fusion(f32[5,32,4,512]{3,2,1,0:T(4,128)S(1)} %copy-done.2, f32[5,32,4,512]{3,2,1,0:T(4,128)S(1)} %copy-done, f32[32,4,512]{2,1,0:T(4,128)S(1)} %get-tuple-element.35, f32[5]{0:T(128)S(1)} %get-tuple-element.24, f32[32,4,512]{2,1,0:T(4,128)S(1)} %get-tuple-element.36, f32[5]{0:T(128)S(1)} %slice_reduce_fusion.1, ...), kind=kLoop, calls=%fused_computation.8 | loop fusion | flops 13762560 | bytes 9437584 | tf_op jit(solution)/shard_map/add | solution.py:107
  322.5 1.5 reshape.78.rhs_ref
  324.0 2.2 gather_fusion.1
  326.3 2.2 gather_fusion.2
  328.5 1.9 fusion.1
  330.4 6.2 %gather_fusion = bf16[128,25,512]{2,1,0:T(8,128)(2,1)} fusion(bf16[256,25,512]{2,1,0:T(8,128)(2,1)} %all-to-all-done.2, s32[1024]{0:T(1024)S(1)} %pad_clamp_fusion), kind=kCustom, calls=%fused_computation.2 | custom fusion | bytes 6554112 | tf_op jit(solution)/shard_map/jit(_take)/gather | solution.py:122
  336.6 7.9 %fusion.pivot_ref = bf16[25,128,512]{2,1,0:T(8,128)(2,1)} fusion(bf16[128,25,512]{2,1,0:T(8,128)(2,1)} %gather_fusion, pred[128]{0:T(512)(128)(4,1)S(1)} %get-tuple-element.25), kind=kLoop, calls=%fused_computation.5 | loop fusion | flops 1638400 | bytes 6553728 | tf_op jit(solution)/shard_map/jit(_take)/select_n | solution.py:122
  344.4 15.6 %shard_map.91 = f32[5,128,512]{2,1,0:T(8,128)} custom-call(f32[5,128,512]{2,1,0:T(8,128)} %reshape.78.rhs_ref, s32[128,1]{1,0:T(8,128)} %reshape.113.lens_ref, bf16[5,128,512]{2,1,0:T(8,128)(2,1)} %get-tuple-element.54.lower_ref, bf16[5,128,512]{2,1,0:T(8,128)(2,1)} %get-tuple-element.53.upper_ref, bf16[25,128,512]{2,1,0:T(8,128)(2,1)} %fusion.pivot_ref, ...), custom_call_target="tpu_custom_call" | custom-call | tf_op jit(solution)/shard_map/pallas_call | solution.py:71
  360.0 2.6 reshape.82
  (22 shorter events, 0.1 us)
Async XLA Ops:
  3.4 12.3 %copy-start.3 = (bf16[1,256,5,512]{3,1,2,0:T(8,128)(2,1)S(1)}, bf16[1,256,5,512]{3,1,2,0:T(8,128)(2,1)}, u32[]{:S(2)}) copy-start(bf16[1,256,5,512]{3,1,2,0:T(8,128)(2,1)} %param.18) | copy-start | bytes 3932164
  3.4 62.0 %all-to-all-start = ((bf16[256,5,512]{2,1,0:T(8,128)(2,1)}), bf16[256,5,512]{2,1,0:T(8,128)(2,1)S(1)}, u32[]{:S(2)}, u32[]{:S(2)}) async-start(bf16[256,5,512]{2,1,0:T(8,128)(2,1)} %bitcast.68), calls=%async_computation | async-start | bytes 4194304 | tf_op jit(solution)/shard_map/all_to_all | solution.py:116
  65.4 1.3 copy-start.1
  66.7 56.8 %all-to-all-start.1 = ((bf16[256,5,512]{2,1,0:T(8,128)(2,1)}), bf16[256,5,512]{2,1,0:T(8,128)(2,1)}, u32[]{:S(2)}, u32[]{:S(2)}) async-start(bf16[256,5,512]{2,1,0:T(8,128)(2,1)} %bitcast.67), calls=%async_computation.1 | async-start | bytes 4194304 | tf_op jit(solution)/shard_map/all_to_all | solution.py:117
  123.5 7.5 %copy-start = (f32[5,32,4,512]{3,2,1,0:T(4,128)S(1)}, f32[5,32,4,512]{3,2,1,0:T(4,128)}, u32[]{:S(2)}) copy-start(f32[5,32,4,512]{3,2,1,0:T(4,128)} %param.11) | copy-start | bytes 3932164
  123.5 206.9 %all-to-all-start.2 = ((bf16[256,25,512]{2,1,0:T(8,128)(2,1)}), bf16[256,25,512]{2,1,0:T(8,128)(2,1)}, u32[]{:S(2)}, u32[]{:S(2)}) async-start(bf16[256,25,512]{2,1,0:T(8,128)(2,1)} %bitcast.69), calls=%async_computation.2 | async-start | bytes 16777216 | tf_op jit(solution)/shard_map/all_to_all | solution.py:118
  131.0 177.8 %collective-permute-start.1 = (f32[5,1,4,512]{3,2,1,0:T(4,128)S(1)}, f32[5,1,4,512]{3,2,1,0:T(4,128)S(1)}, u32[]{:S(2)}, u32[]{:S(2)}) collective-permute-start(f32[5,1,4,512]{3,2,1,0:T(4,128)S(1)} %get-tuple-element.48), channel_id=1, source_target_pairs={{0,4},{4,8},{8,12},{12,16},{16,20},{20,24},{24,28},{28,32},{32,36}... | collective-permute-start | bytes 122888 | tf_op jit(solution)/shard_map/ppermute | solution.py:18
  132.5 6.1 %copy-start.6 = (s32[1,32,4,1]{1,3,2,0:T(1,128)S(1)}, s32[1,32,4,1]{1,3,2,0:T(1,128)}, u32[]{:S(2)}) copy-start(s32[1,32,4,1]{1,3,2,0:T(1,128)} %param.15) | copy-start | bytes 1540
  132.5 6.7 %copy-start.5 = (f32[4,5,5]{2,0,1:T(4,128)S(1)}, f32[4,5,5]{2,0,1:T(4,128)}, u32[]{:S(2)}) copy-start(f32[4,5,5]{2,0,1:T(4,128)} %param.16) | copy-start | bytes 1204
  132.5 182.0 %collective-permute-start = (f32[5,1,4,512]{3,2,1,0:T(4,128)S(1)}, f32[5,1,4,512]{3,2,1,0:T(4,128)S(1)}, u32[]{:S(2)}, u32[]{:S(2)}) collective-permute-start(f32[5,1,4,512]{3,2,1,0:T(4,128)S(1)} %get-tuple-element.47), channel_id=1, source_target_pairs={{4,0},{8,4},{12,8},{16,12},{20,16},{24,20},{28,24},{32,28},{36,32}... | collective-permute-start | bytes 122888 | tf_op jit(solution)/shard_map/ppermute | solution.py:21
  133.0 181.9 %collective-permute-start.2 = (f32[5,32,1,512]{3,1,2,0:T(8,128)S(1)}, f32[5,32,1,512]{3,1,2,0:T(8,128)S(1)}, u32[]{:S(2)}, u32[]{:S(2)}) collective-permute-start(f32[5,32,1,512]{3,1,2,0:T(8,128)S(1)} %copy.52), channel_id=1, source_target_pairs={{1,0},{2,1},{3,2},{5,4},{6,5},{7,6},{9,8},{10,9},{11,10},{13,12},{... | collective-permute-start | bytes 983048 | tf_op jit(solution)/shard_map/ppermute | solution.py:21
  134.4 181.0 %collective-permute-start.3 = (f32[5,32,1,512]{3,1,2,0:T(8,128)S(1)}, f32[5,32,1,512]{3,1,2,0:T(8,128)S(1)}, u32[]{:S(2)}, u32[]{:S(2)}) collective-permute-start(f32[5,32,1,512]{3,1,2,0:T(8,128)S(1)} %copy.53), channel_id=1, source_target_pairs={{0,1},{1,2},{2,3},{4,5},{5,6},{6,7},{8,9},{9,10},{10,11},{12,13},{... | collective-permute-start | bytes 983048 | tf_op jit(solution)/shard_map/ppermute | solution.py:18
  139.8 1.5 copy-start.7
  316.4 1.3 copy-start.2
  316.4 1.3 copy-start.4
where the time goes:
time: 364 us; the launch traced here: 363 us
  waiting for transfers between devices  259 us (71%)
  local copies, waits for them, and re-layouts  37.9 us (10%)
  starting transfers between devices  34 us (9%)
  other arithmetic  16.1 us (4%)
  Pallas kernels  15.6 us (4%)
    ppermute x2, waiting for transfers between devices, extended(): lax.ppermute(lax.slice_in_dim(block, block.shape[dim] - width, None, axis...  167 us
    all_to_all x1, waiting for transfers between devices, per_device(): lax.all_to_all(lower_coef[0], 'circ', split_axis=0, concat_axis=0, tiled=...  47.5 us
    all_to_all x1, waiting for transfers between devices, per_device(): lax.all_to_all(upper_coef[0], 'circ', split_axis=0, concat_axis=0, tiled=...  39.5 us
    unnamed x25, local copies, waits for them, and re-layouts  18.4 us
    pallas_call x1, Pallas kernels, line_solve(): pl.pallas_call(solve_kernel, out_shape=jax.ShapeDtypeStruct(rhs.shape, jn...  15.6 us
    all_to_all x1, starting transfers between devices, per_device(): lax.all_to_all(lower_coef[0], 'circ', split_axis=0, concat_axis=0, tiled=...  12.3 us
    select_n x2, other arithmetic, per_device(): pivot_rows = jnp.take(pivot_here, slot_ids, axis=0).transpose(1, 0, 2)  7.89 us
    all_to_all x1, starting transfers between devices, per_device(): lax.all_to_all(pivot_inverse[0], 'circ', split_axis=0, concat_axis=0, til...  7.45 us
  transfers between devices with their start and end apart: 7, of which 4 were waited for; matrix products, arithmetic and copies ran while one was open for 9% of the time, Pallas kernels for 0%

commit v1 on v0

--- a/solution.py
+++ b/solution.py
@@ -45,12 +45,13 @@
     return value
 
 
-def solve_kernel(rhs_ref, lens_ref, lower_ref, upper_ref, pivot_ref, adj_ref, out_ref):
+def solve_kernel(rhs_ref, lower_ref, upper_ref, pivot_ref, out_ref):
     fields, rows, points = rhs_ref.shape
     pos = lax.broadcasted_iota(jnp.int32, (fields, rows, points), 2)
-    active = pos < lens_ref[...][None, :, :]
+    rhs = rhs_ref[...]
+    active = rhs == rhs
     forward_coef = jnp.where(active, -lower_ref[...].astype(jnp.float32), 0.0)
-    interim = scan_forward(forward_coef, jnp.where(active, rhs_ref[...], 0.0), pos)
+    interim = scan_forward(forward_coef, jnp.where(active, rhs, 0.0), pos)
     applied = []
     for f in range(fields):
         total = pivot_ref[f * fields].astype(jnp.float32) * interim[0]
@@ -59,11 +60,10 @@
         applied.append(total)
     applied = jnp.stack(applied, axis=0)
     backward_coef = jnp.where(active, -upper_ref[...].astype(jnp.float32), 0.0)
-    solved = scan_backward(backward_coef, jnp.where(active, applied, 0.0), pos)
-    out_ref[...] = adj_ref[...] + solved
+    out_ref[...] = scan_backward(backward_coef, jnp.where(active, applied, 0.0), pos)
 
 
-def line_solve(rhs, lens, lower, upper, pivot, adj, block_rows=16):
+def line_solve(rhs, lower, upper, pivot, block_rows=16):
     fields, lines, points = rhs.shape
     blocks = pivot.shape[0]
     grid = (lines // block_rows,)
@@ -74,14 +74,12 @@
         grid=grid,
         in_specs=[
             field_spec,
-            pl.BlockSpec((block_rows, 1), lambda i: (i, 0)),
             field_spec,
             field_spec,
             pl.BlockSpec((blocks, block_rows, points), lambda i: (0, i, 0)),
-            field_spec,
         ],
         out_specs=field_spec,
-    )(rhs, lens, lower, upper, pivot, adj)
+    )(rhs, lower, upper, pivot)
 
 
 def per_device(
@@ -91,6 +89,7 @@
     line_count = circ_cells * axial_cells
     circ_devices = lax.axis_size("circ")
     capacity = 2 * line_count // circ_devices
+    slot_count = lower_coef.shape[1]
     circ_padded = extended(adjoint, (("circ", 1),), 1, True)
     axial_padded = extended(adjoint, (("ax", 2),), 1, False)
     neighbours = (
@@ -105,23 +104,30 @@
             term = coupling[k, :, g][:, None, None, None] * near[g][None]
             coupled = term if coupled is None else coupled + term
     residual = source - adjoint + step_size[None] * coupled
+    active = jnp.arange(points)[None, None, None, :] < lengths[None, :, :, None]
+    residual = jnp.where(active, residual, jnp.nan)
     line_rhs = residual.reshape(fields, line_count, points)
-    line_adj = adjoint.reshape(fields, line_count, points)
-    line_lens = lengths.reshape(line_count, 1)
     targets = line_owner.reshape(line_count)
     ordinal = jnp.arange(line_count)
     earlier_same = (targets[:, None] == targets[None, :]) & (ordinal[None, :] < ordinal[:, None])
     slot_ids = targets * capacity + jnp.sum(earlier_same, axis=1)
-    lower_here, upper_here, pivot_here = (
-        lax.all_to_all(lower_coef[0], "circ", split_axis=0, concat_axis=0, tiled=True),
-        lax.all_to_all(upper_coef[0], "circ", split_axis=0, concat_axis=0, tiled=True),
-        lax.all_to_all(pivot_inverse[0], "circ", split_axis=0, concat_axis=0, tiled=True),
+    line_of_slot = jnp.full((slot_count,), line_count, jnp.int32).at[slot_ids].set(
+        ordinal.astype(jnp.int32)
     )
-    lower_rows = jnp.take(lower_here, slot_ids, axis=0).transpose(1, 0, 2)
-    upper_rows = jnp.take(upper_here, slot_ids, axis=0).transpose(1, 0, 2)
-    pivot_rows = jnp.take(pivot_here, slot_ids, axis=0).transpose(1, 0, 2)
-    updated = line_solve(line_rhs, line_lens, lower_rows, upper_rows, pivot_rows, line_adj)
-    return updated.reshape(fields, circ_cells, axial_cells, points)
+    padded_rhs = jnp.concatenate(
+        [line_rhs, jnp.full((fields, 1, points), jnp.nan, jnp.float32)], axis=1
+    )
+    outgoing = jnp.take(padded_rhs, line_of_slot, axis=1)
+    owned_rhs = lax.all_to_all(outgoing, "circ", split_axis=1, concat_axis=1, tiled=True)
+    owned_solution = line_solve(
+        owned_rhs,
+        lower_coef[0].transpose(1, 0, 2),
+        upper_coef[0].transpose(1, 0, 2),
+        pivot_inverse[0].transpose(1, 0, 2),
+    )
+    returned = lax.all_to_all(owned_solution, "circ", split_axis=1, concat_axis=1, tiled=True)
+    correction = jnp.take(returned, slot_ids, axis=1)
+    return adjoint + correction.reshape(fields, circ_cells, axial_cells, points)
 
 
 def solution(mesh):

time: 364 us -> 283 us (0.78)
  waiting for transfers between devices: 259 us -> 95.1 us
  blocking collectives: 0 us -> 107 us
  starting transfers between devices: 34 us -> 14.5 us
  local copies, waits for them, and re-layouts: 37.9 us -> 23.5 us
  Pallas kernels: 15.6 us -> 26.9 us
  other arithmetic: 16.1 us -> 11.5 us
    ppermute x2, waiting for transfers between devices: 167 us -> 0.01 us  [extended(): lax.ppermute(lax.slice_in_dim(block, block.shape[dim] - width, None, axis...]
    all_to_all x0 -> x1, blocking collectives: none -> 107 us  [per_device(): lax.all_to_all(outgoing, 'circ', split_axis=1, concat_axis=1, tiled=True)]
    all_to_all x3 -> x1, starting transfers between devices: 27 us -> 7.25 us  [per_device(): lax.all_to_all(owned_solution, 'circ', split_axis=1, concat_axis=1, tiled...]
    unnamed x25 -> x18, local copies, waits for them, and re-layouts: 18.4 us -> 1.49 us
    pallas_call x1, Pallas kernels: 15.6 us -> 26.9 us  [line_solve(): pl.pallas_call(solve_kernel, out_shape=jax.ShapeDtypeStruct(rhs.shape, jn...]
    all_to_all x3 -> x1, waiting for transfers between devices: 87 us -> 93.4 us  [per_device(): lax.all_to_all(owned_solution, 'circ', split_axis=1, concat_axis=1, tiled...]
    reshape x4 -> x0, local copies, waits for them, and re-layouts: 6.32 us -> none  [the longest x1 2.6 us: per_device(): return updated.reshape(fields, circ_cells, axial_cells, points)]
    pallas_call x0 -> x1, local copies, waits for them, and re-layouts: none -> 5.28 us  [line_solve(): pl.pallas_call(solve_kernel, out_shape=jax.ShapeDtypeStruct(rhs.shape, jn...]
  transfers between devices with their start and end apart: 7 -> 5, of which waited for: 4 -> 2; matrix products, arithmetic and copies ran while one was open for 9% -> 3% of each run, Pallas kernels for 0% -> 0%
where the time goes in v1:
time: 283 us; the launch traced here: 279 us
  blocking collectives  107 us (38%)
  waiting for transfers between devices  95.1 us (34%)
  Pallas kernels  26.9 us (10%)
  local copies, waits for them, and re-layouts  23.5 us (8%)
  starting transfers between devices  14.5 us (5%)
  other arithmetic  11.5 us (4%)
    all_to_all x1, blocking collectives, per_device(): lax.all_to_all(outgoing, 'circ', split_axis=1, concat_axis=1, tiled=True)  107 us
    all_to_all x1, waiting for transfers between devices, per_device(): lax.all_to_all(owned_solution, 'circ', split_axis=1, concat_axis=1, tiled...  93.4 us
    pallas_call x1, Pallas kernels, line_solve(): pl.pallas_call(solve_kernel, out_shape=jax.ShapeDtypeStruct(rhs.shape, jn...  26.9 us
    all_to_all x1, starting transfers between devices, per_device(): lax.all_to_all(owned_solution, 'circ', split_axis=1, concat_axis=1, tiled...  7.25 us
    ppermute x2, starting transfers between devices, extended(): lax.ppermute(lax.slice_in_dim(block, block.shape[dim] - width, None, axis...  5.86 us
  transfers between devices with their start and end apart: 5, of which 2 were waited for; matrix products, arithmetic and copies ran while one was open for 3% of the time, Pallas kernels for 0%

profile of v1, /device:TPU:25, one launch (start us, length us, event | category | flops | bytes accessed | tf_op | source)
XLA Modules:
  0.0 278.8 jit_solution(4235950890640834244)
XLA Ops:
  0.0 0.8 fusion.7
  0.8 1.9 collective-permute-start.1
  2.7 0.1 collective-permute-start
  2.8 2.6 fusion.8
  5.4 1.3 collective-permute-start.2
  6.7 4.0 %collective-permute-start.3 = (f32[5,32,1,512]{3,1,2,0:T(8,128)S(1)}, f32[5,32,1,512]{3,1,2,0:T(8,128)S(1)}, u32[]{:S(2)}, u32[]{:S(2)}) collective-permute-start(f32[5,32,1,512]{3,1,2,0:T(8,128)S(1)} %copy.51), channel_id=1, source_target_pairs={{0,1},{1,2},{2,3},{4,5},{5,6},{6,7},{8,9},{9,10},{10,11},{12,13},{... | collective-permute-start | bytes 983048 | tf_op jit(solution)/shard_map/ppermute | solution.py:18
  10.7 0.0 copy-done.3
  10.7 0.4 slice_reduce_fusion.19
  11.1 0.2 slice_reduce_fusion.1
  11.3 0.1 copy.37
  11.4 0.1 copy.40
  11.5 0.1 mul.373
  11.6 0.1 reshape.84
  11.7 0.2 convert_reduce_fusion
  11.9 1.2 scatter_custom_fusion
  13.1 0.1 copy.41
  13.2 0.1 iota_compare_fusion
  13.3 0.0 collective-permute-done.1
  13.4 0.5 constant_dynamic-update-slice_fusion.1
  13.9 0.0 collective-permute-done
  13.9 0.2 slice_bitcast_fusion.9
  14.2 0.2 slice_bitcast_fusion.4
  14.4 1.7 collective-permute-done.2
  16.1 0.3 copy.43
  16.5 0.8 maximum_bitcast_fusion.7
  17.2 0.0 collective-permute-done.3
  17.2 0.3 copy.45
  17.6 0.0 copy-start.1
  17.6 0.0 copy-start.2
  17.6 0.6 maximum_bitcast_fusion.3
  18.2 0.7 copy-done.1
  18.9 0.0 copy-done.2
  18.9 5.0 %add_select_fusion = f32[5,32,4,512]{3,2,1,0:T(4,128)S(1)} fusion(f32[5,32,4,512]{3,2,1,0:T(4,128)S(1)} %copy-done.1, f32[5,32,4,512]{3,2,1,0:T(4,128)S(1)} %copy-done, f32[32,4,512]{2,1,0:T(4,128)S(1)} %get-tuple-element.32, f32[5]{0:T(128)S(1)} %get-tuple-element.23, f32[32,4,512]{2,1,0:T(4,128)S(1)} %get-tuple-element.33, f32[5]{0:T(128)S(1)} %slice_reduce_fusion.1, ...), kind=kLoop, calls=%fused_computation.6 | loop fusion | flops 14090240 | bytes 9503120 | tf_op jit(solution)/shard_map/jit(_where)/select_n | solution.py:108
  23.9 0.8 copy.46
  24.8 0.2 concatenate.21
  25.0 3.0 %gather_fusion = f32[256,5,512]{2,1,0:T(8,128)} fusion(f32[5,129,512]{2,0,1:T(8,128)S(1)} %concatenate.21, s32[1024]{0:T(1024)S(1)} %pad_clamp_fusion.1), kind=kCustom, calls=%fused_computation | custom fusion | bytes 5243904 | tf_op jit(solution)/shard_map/jit(_take)/gather | solution.py:120
  28.0 2.7 select_bitcast_fusion
  30.7 107.0 %all_to_all.10 = f32[5,256,512]{2,0,1:T(8,128)S(1)} all-to-all(f32[5,256,512]{2,0,1:T(8,128)S(1)} %select_bitcast_fusion), channel_id=1, replica_groups=mesh['circ'=64,'ax'=4] {'circ'}, dimensions={1} | all-to-all | bytes 5242880 | tf_op jit(solution)/shard_map/all_to_all | solution.py:121
  137.7 3.0 %copy.47.rhs_ref = f32[5,256,512]{2,1,0:T(8,128)} copy(f32[5,256,512]{2,0,1:T(8,128)S(1)} %all_to_all.10) | data formatting | bytes 5242880 | tf_op jit(solution)/shard_map/all_to_all | solution.py:121
  140.7 26.9 %shard_map.91 = f32[5,256,512]{2,1,0:T(8,128)} custom-call(f32[5,256,512]{2,1,0:T(8,128)} %copy.47.rhs_ref, bf16[5,256,512]{2,1,0:T(8,128)(2,1)} %bitcast.73, bf16[5,256,512]{2,1,0:T(8,128)(2,1)} %bitcast.74, bf16[25,256,512]{2,1,0:T(8,128)(2,1)} %bitcast.71), custom_call_target="tpu_custom_call" | custom-call | tf_op jit(solution)/shard_map/pallas_call | solution.py:71
  167.5 5.3 %copy.48 = f32[5,256,512]{2,0,1:T(8,128)} copy(f32[5,256,512]{2,1,0:T(8,128)} %shard_map.91) | data formatting | bytes 5242880 | tf_op jit(solution)/shard_map/pallas_call | solution.py:71
  172.8 7.2 %all-to-all-start.1 = ((f32[5,256,512]{2,0,1:T(8,128)}), f32[5,256,512]{2,0,1:T(8,128)}, u32[]{:S(2)}, u32[]{:S(2)}) async-start(f32[5,256,512]{2,0,1:T(8,128)} %copy.48), calls=%async_computation.1 | async-start | bytes 8388608 | tf_op jit(solution)/shard_map/all_to_all | solution.py:128
  180.1 0.1 reduce_sum.14
  180.2 0.1 copy.38
  180.3 0.1 copy.39
  180.4 93.4 %all-to-all-done.1 = f32[5,256,512]{2,0,1:T(8,128)} async-done(((f32[5,256,512]{2,0,1:T(8,128)}), f32[5,256,512]{2,0,1:T(8,128)}, u32[]{:S(2)}, u32[]{:S(2)}) %all-to-all-start.1) | async-done | bytes 2621472 | tf_op jit(solution)/shard_map/all_to_all | solution.py:128
  273.8 2.9 %gather_fusion.1 = f32[128,5,512]{2,1,0:T(8,128)S(1)} fusion(f32[5,256,512]{2,0,1:T(8,128)} %all-to-all-done.1, s32[1024]{0:T(1024)S(1)} %pad_clamp_fusion), kind=kCustom, calls=%fused_computation.1 | custom fusion | bytes 2621952 | tf_op jit(solution)/shard_map/jit(_take)/gather | solution.py:129
  276.7 2.1 fusion
  (19 shorter events, 0.1 us)
Async XLA Ops:
  0.8 12.5 %collective-permute-start.1 = (f32[5,1,4,512]{3,2,1,0:T(4,128)S(1)}, f32[5,1,4,512]{3,2,1,0:T(4,128)S(1)}, u32[]{:S(2)}, u32[]{:S(2)}) collective-permute-start(f32[5,1,4,512]{3,2,1,0:T(4,128)S(1)} %get-tuple-element.45), channel_id=1, source_target_pairs={{0,4},{4,8},{8,12},{12,16},{16,20},{20,24},{24,28},{28,32},{32,36}... | collective-permute-start | bytes 122888 | tf_op jit(solution)/shard_map/ppermute | solution.py:18
  2.7 8.1 %copy-start.3 = (f32[4,5,5]{2,0,1:T(4,128)S(1)}, f32[4,5,5]{2,0,1:T(4,128)}, u32[]{:S(2)}) copy-start(f32[4,5,5]{2,0,1:T(4,128)} %param.14) | copy-start | bytes 1204
  2.7 8.6 %copy-start.4 = (s32[1,32,4,1]{1,3,2,0:T(1,128)S(1)}, s32[1,32,4,1]{1,3,2,0:T(1,128)}, u32[]{:S(2)}) copy-start(s32[1,32,4,1]{1,3,2,0:T(1,128)} %param.13) | copy-start | bytes 1540
  2.7 10.4 %copy-start.5 = (s32[32,4]{0,1:T(4,128)S(1)}, s32[32,4]{0,1:T(4,128)}, u32[]{:S(2)}) copy-start(s32[32,4]{0,1:T(4,128)} %param.12) | copy-start | bytes 1540
  2.7 10.7 %copy-start = (f32[5,32,4,512]{3,2,1,0:T(4,128)S(1)}, f32[5,32,4,512]{3,2,1,0:T(4,128)}, u32[]{:S(2)}) copy-start(f32[5,32,4,512]{3,2,1,0:T(4,128)} %param.9) | copy-start | bytes 3932164
  2.7 11.2 %collective-permute-start = (f32[5,1,4,512]{3,2,1,0:T(4,128)S(1)}, f32[5,1,4,512]{3,2,1,0:T(4,128)S(1)}, u32[]{:S(2)}, u32[]{:S(2)}) collective-permute-start(f32[5,1,4,512]{3,2,1,0:T(4,128)S(1)} %get-tuple-element.44), channel_id=1, source_target_pairs={{4,0},{8,4},{12,8},{16,12},{20,16},{24,20},{28,24},{32,28},{36,32}... | collective-permute-start | bytes 122888 | tf_op jit(solution)/shard_map/ppermute | solution.py:21
  5.4 10.7 %collective-permute-start.2 = (f32[5,32,1,512]{3,1,2,0:T(8,128)S(1)}, f32[5,32,1,512]{3,1,2,0:T(8,128)S(1)}, u32[]{:S(2)}, u32[]{:S(2)}) collective-permute-start(f32[5,32,1,512]{3,1,2,0:T(8,128)S(1)} %copy.50), channel_id=1, source_target_pairs={{1,0},{2,1},{3,2},{5,4},{6,5},{7,6},{9,8},{10,9},{11,10},{13,12},{... | collective-permute-start | bytes 983048 | tf_op jit(solution)/shard_map/ppermute | solution.py:21
  6.7 10.5 %collective-permute-start.3 = (f32[5,32,1,512]{3,1,2,0:T(8,128)S(1)}, f32[5,32,1,512]{3,1,2,0:T(8,128)S(1)}, u32[]{:S(2)}, u32[]{:S(2)}) collective-permute-start(f32[5,32,1,512]{3,1,2,0:T(8,128)S(1)} %copy.51), channel_id=1, source_target_pairs={{0,1},{1,2},{2,3},{4,5},{5,6},{6,7},{8,9},{9,10},{10,11},{12,13},{... | collective-permute-start | bytes 983048 | tf_op jit(solution)/shard_map/ppermute | solution.py:18
  17.6 1.3 copy-start.1
  17.6 1.3 copy-start.2
  172.8 101.0 %all-to-all-start.1 = ((f32[5,256,512]{2,0,1:T(8,128)}), f32[5,256,512]{2,0,1:T(8,128)}, u32[]{:S(2)}, u32[]{:S(2)}) async-start(f32[5,256,512]{2,0,1:T(8,128)} %copy.48), calls=%async_computation.1 | async-start | bytes 8388608 | tf_op jit(solution)/shard_map/all_to_all | solution.py:128

commit v2 on v1

--- a/solution.py
+++ b/solution.py
@@ -82,6 +82,91 @@
     )(rhs, lower, upper, pivot)
 
 
+MESH = pl.DeviceIdType.MESH
+
+
+def exchange_kernel(x_ref, o_ref, send_sems, recv_sems, local_sem):
+    peers = x_ref.shape[0]
+    me = lax.axis_index("circ")
+    plane = lax.axis_index("ax")
+    barrier = pltpu.get_barrier_semaphore()
+
+    def greet(i, carry):
+        peer = lax.rem(me + i, peers)
+        pl.semaphore_signal(barrier, inc=1, device_id=(peer, plane), device_id_type=MESH)
+        return carry
+
+    lax.fori_loop(1, peers, greet, 0)
+    pl.semaphore_wait(barrier, peers - 1)
+    local = pltpu.make_async_copy(x_ref.at[me], o_ref.at[me], local_sem)
+    local.start()
+
+    def outgoing(i):
+        peer = lax.rem(me + i, peers)
+        return pltpu.make_async_remote_copy(
+            src_ref=x_ref.at[peer],
+            dst_ref=o_ref.at[me],
+            send_sem=send_sems.at[peer],
+            recv_sem=recv_sems.at[me],
+            device_id=(peer, plane),
+            device_id_type=MESH,
+        )
+
+    def incoming(i):
+        peer = lax.rem(me + peers - i, peers)
+        return pltpu.make_async_remote_copy(
+            src_ref=x_ref.at[me],
+            dst_ref=o_ref.at[peer],
+            send_sem=send_sems.at[me],
+            recv_sem=recv_sems.at[peer],
+            device_id=(peer, plane),
+            device_id_type=MESH,
+        )
+
+    def start(i, carry):
+        outgoing(i).start()
+        return carry
+
+    def finish(i, carry):
+        outgoing(i).wait_send()
+        incoming(i).wait_recv()
+        return carry
+
+    lax.fori_loop(1, peers, start, 0)
+    local.wait()
+    lax.fori_loop(1, peers, finish, 0)
+
+
+def exchange(chunks, collective_id):
+    peers = chunks.shape[0]
+    return pl.pallas_call(
+        exchange_kernel,
+        out_shape=jax.ShapeDtypeStruct(chunks.shape, chunks.dtype),
+        in_specs=[pl.BlockSpec(memory_space=pl.ANY)],
+        out_specs=pl.BlockSpec(memory_space=pl.ANY),
+        scratch_shapes=[
+            pltpu.SemaphoreType.DMA((peers,)),
+            pltpu.SemaphoreType.DMA((peers,)),
+            pltpu.SemaphoreType.DMA(()),
+        ],
+        compiler_params=pltpu.CompilerParams(collective_id=collective_id, has_side_effects=True),
+    )(chunks)
+
+
+def to_chunks(rows, peers):
+    fields, slots, points = rows.shape
+    per_peer = slots // peers
+    flat = rows.reshape(fields, peers, per_peer, points).transpose(1, 0, 2, 3)
+    return flat.reshape(peers, fields * per_peer * points // 128, 128)
+
+
+def from_chunks(chunks, fields, points):
+    peers = chunks.shape[0]
+    per_peer = chunks.shape[1] * 128 // (fields * points)
+    rows = chunks.reshape(peers, fields, per_peer, points).transpose(1, 0, 2, 3)
+    return rows.reshape(fields, peers * per_peer, points)
+
+
 def per_device(
     adjoint, source, step_size, lengths, line_owner, coupling, lower_coef, upper_coef, pivot_inverse
 ):
@@ -118,14 +203,14 @@
         [line_rhs, jnp.full((fields, 1, points), jnp.nan, jnp.float32)], axis=1
     )
     outgoing = jnp.take(padded_rhs, line_of_slot, axis=1)
-    owned_rhs = lax.all_to_all(outgoing, "circ", split_axis=1, concat_axis=1, tiled=True)
+    owned_rhs = from_chunks(exchange(to_chunks(outgoing, circ_devices), 0), fields, points)
     owned_solution = line_solve(
         owned_rhs,
         lower_coef[0].transpose(1, 0, 2),
         upper_coef[0].transpose(1, 0, 2),
         pivot_inverse[0].transpose(1, 0, 2),
     )
-    returned = lax.all_to_all(owned_solution, "circ", split_axis=1, concat_axis=1, tiled=True)
+    returned = from_chunks(exchange(to_chunks(owned_solution, circ_devices), 1), fields, points)
     correction = jnp.take(returned, slot_ids, axis=1)
     return adjoint + correction.reshape(fields, circ_cells, axial_cells, points)
 

time: 283 us -> 249 us (0.88)
  Pallas kernels: 26.9 us -> 170 us
  blocking collectives: 107 us -> 0 us
  waiting for transfers between devices: 95.1 us -> 1.27 us
  local copies, waits for them, and re-layouts: 23.5 us -> 54.2 us
  starting transfers between devices: 14.5 us -> 7.24 us
    pallas_call x0 -> x2, Pallas kernels: none -> 143 us  [exchange(): pl.pallas_call(exchange_kernel, out_shape=jax.ShapeDtypeStruct(chunks.sha...]
    all_to_all x1 -> x0, blocking collectives: 107 us -> none  [per_device(): lax.all_to_all(outgoing, 'circ', split_axis=1, concat_axis=1, tiled=True)]
    all_to_all x1 -> x0, waiting for transfers between devices: 93.4 us -> none  [per_device(): lax.all_to_all(owned_solution, 'circ', split_axis=1, concat_axis=1, tiled...]
    reshape x0 -> x9, local copies, waits for them, and re-layouts: none -> 36.7 us  [the longest x3 11.8 us: from_chunks(): rows = chunks.reshape(peers, fields, per_peer, points).transpose(1, 0, 2, 3)]
    all_to_all x1 -> x0, starting transfers between devices: 7.25 us -> none  [per_device(): lax.all_to_all(owned_solution, 'circ', split_axis=1, concat_axis=1, tiled...]
    pallas_call x1 -> x0, local copies, waits for them, and re-layouts: 5.28 us -> none  [line_solve(): pl.pallas_call(solve_kernel, out_shape=jax.ShapeDtypeStruct(rhs.shape, jn...]
    transpose x0 -> x1, other arithmetic: none -> 4.23 us  [to_chunks(): flat = rows.reshape(fields, peers, per_peer, points).transpose(1, 0, 2, 3)]
    all_to_all x1 -> x0, local copies, waits for them, and re-layouts: 3.02 us -> none  [per_device(): lax.all_to_all(outgoing, 'circ', split_axis=1, concat_axis=1, tiled=True)]
  transfers between devices with their start and end apart: 5 -> 4, of which waited for: 2 -> 1; matrix products, arithmetic and copies ran while one was open for 3% -> 3% of each run, Pallas kernels for 0% -> 0%
where the time goes in v2:
time: 249 us; the launch traced here: 246 us
  Pallas kernels  170 us (68%)
  local copies, waits for them, and re-layouts  54.2 us (22%)
  other arithmetic  13 us (5%)
  starting transfers between devices  7.24 us (3%)
    pallas_call x2, Pallas kernels, exchange(): pl.pallas_call(exchange_kernel, out_shape=jax.ShapeDtypeStruct(chunks.sha...  143 us
    pallas_call x1, Pallas kernels, line_solve(): pl.pallas_call(solve_kernel, out_shape=jax.ShapeDtypeStruct(rhs.shape, jn...  26.8 us
    reshape x3, local copies, waits for them, and re-layouts, from_chunks(): rows = chunks.reshape(peers, fields, per_peer, points).transpose(1, 0, 2, 3)  11.8 us
    reshape x2, local copies, waits for them, and re-layouts, from_chunks(): return rows.reshape(fields, peers * per_peer, points)  9.03 us
    reshape x2, local copies, waits for them, and re-layouts, to_chunks(): return flat.reshape(peers, fields * per_peer * points // 128, 128)  8.2 us
    reshape x2, local copies, waits for them, and re-layouts, to_chunks(): flat = rows.reshape(fields, peers, per_peer, points).transpose(1, 0, 2, 3)  7.66 us
    ppermute x2, starting transfers between devices, extended(): lax.ppermute(lax.slice_in_dim(block, block.shape[dim] - width, None, axis...  5.86 us
    select_n x1, other arithmetic, per_device(): residual = jnp.where(active, residual, jnp.nan)  5 us
  transfers between devices with their start and end apart: 4, of which 1 were waited for; matrix products, arithmetic and copies ran while one was open for 3% of the time, Pallas kernels for 0%

profile of v2, /device:TPU:25, one launch (start us, length us, event | category | flops | bytes accessed | tf_op | source)
XLA Modules:
  0.0 245.8 jit_solution(17890476225214756627)
XLA Ops:
  0.0 0.8 fusion.8
  0.8 1.9 collective-permute-start.1
  2.7 0.1 collective-permute-start
  2.8 2.6 %fusion.9 = (f32[5,32,1,512]{3,2,1,0:T(1,128)S(1)}, f32[5,32,1,512]{3,2,1,0:T(1,128)S(1)}) fusion(f32[5,32,4,512]{3,2,1,0:T(4,128)} %param.9), kind=kLoop, calls=%fused_computation.73 | loop fusion | bytes 1310720 | tf_op jit(solution)/shard_map/slice | solution.py:21
  5.4 1.3 collective-permute-start.2
  6.7 4.0 %collective-permute-start.3 = (f32[5,32,1,512]{3,1,2,0:T(8,128)S(1)}, f32[5,32,1,512]{3,1,2,0:T(8,128)S(1)}, u32[]{:S(2)}, u32[]{:S(2)}) collective-permute-start(f32[5,32,1,512]{3,1,2,0:T(8,128)S(1)} %copy.68), channel_id=1, source_target_pairs={{0,1},{1,2},{2,3},{4,5},{5,6},{6,7},{8,9},{9,10},{10,11},{12,13},{... | collective-permute-start | bytes 983048 | tf_op jit(solution)/shard_map/ppermute | solution.py:18
  10.7 0.4 slice_reduce_fusion.19
  11.1 0.2 slice_reduce_fusion.1
  11.3 0.1 copy.47
  11.4 0.1 copy.50
  11.5 0.1 mul.373
  11.6 0.1 reshape.109
  11.7 0.2 convert_reduce_fusion
  11.9 1.2 scatter_custom_fusion
  13.1 0.1 reduce_sum.14
  13.2 0.1 copy.51
  13.3 0.1 iota_compare_fusion
  13.5 0.1 broadcast_in_dim.46
  13.7 0.1 copy.49
  13.8 0.5 constant_dynamic-update-slice_fusion.1
  14.3 0.2 slice_bitcast_fusion.9
  14.6 0.2 slice_bitcast_fusion.4
  14.8 1.3 collective-permute-done.2
  16.1 0.3 copy.53
  16.5 0.8 maximum_bitcast_fusion.7
  17.2 0.3 copy.55
  17.6 0.6 maximum_bitcast_fusion.3
  18.2 0.7 copy-done.1
  18.9 5.0 %add_select_fusion = f32[5,32,4,512]{3,2,1,0:T(4,128)S(1)} fusion(f32[5,32,4,512]{3,2,1,0:T(4,128)S(1)} %copy-done.1, f32[5,32,4,512]{3,2,1,0:T(4,128)S(1)} %copy-done, f32[32,4,512]{2,1,0:T(4,128)S(1)} %get-tuple-element.32, f32[5]{0:T(128)S(1)} %get-tuple-element.23, f32[32,4,512]{2,1,0:T(4,128)S(1)} %get-tuple-element.33, f32[5]{0:T(128)S(1)} %slice_reduce_fusion.1, ...), kind=kLoop, calls=%fused_computation.9 | loop fusion | flops 14090240 | bytes 9503120 | tf_op jit(solution)/shard_map/jit(_where)/select_n | solution.py:193
  23.9 0.8 copy.56
  24.7 0.2 concatenate.21
  25.0 3.0 %gather_fusion = f32[256,5,512]{2,1,0:T(8,128)} fusion(f32[5,129,512]{2,0,1:T(8,128)S(1)} %concatenate.21, s32[1024]{0:T(1024)S(1)} %get-tuple-element.51), kind=kCustom, calls=%fused_computation | custom fusion | bytes 5243904 | tf_op jit(solution)/shard_map/jit(_take)/gather | solution.py:205
  28.0 4.2 %fusion = f32[64,5,4,512]{3,2,0,1:T(4,128)S(1)} fusion(f32[5,64,4,512]{3,0,2,1:T(8,128)} %bitcast.82, pred[64,4]{1,0:T(8,128)(4,1)S(1)} %broadcast_in_dim.46), kind=kLoop, calls=%fused_computation.4 | loop fusion | flops 655360 | bytes 5243136 | tf_op jit(solution)/shard_map/transpose | solution.py:159
  32.2 2.2 copy.58
  34.4 4.1 %reshape.111.x_ref = f32[64,80,128]{2,1,0:T(8,128)} reshape(f32[64,5,4,512]{3,2,1,0:T(4,128)} %copy.58) | data formatting | bytes 5242880 | tf_op jit(solution)/shard_map/reshape | solution.py:160
  38.5 71.8 %shard_map.91 = f32[64,80,128]{2,1,0:T(8,128)} custom-call(f32[64,80,128]{2,1,0:T(8,128)} %reshape.111.x_ref), custom_call_target="tpu_custom_call" | custom-call | tf_op jit(solution)/shard_map/pallas_call | solution.py:142
  110.3 4.0 %reshape.112 = f32[64,5,4,512]{3,2,1,0:T(4,128)} reshape(f32[64,80,128]{2,1,0:T(8,128)} %shard_map.91) | data formatting | bytes 5242880 | tf_op jit(solution)/shard_map/reshape | solution.py:166
  114.3 3.8 %copy.78 = f32[64,5,4,512]{3,2,0,1:T(4,128)} copy(f32[64,5,4,512]{3,2,1,0:T(4,128)} %reshape.112) | data formatting | bytes 5242880 | tf_op jit(solution)/shard_map/reshape | solution.py:166
  118.1 4.0 %reshape.113.rhs_ref = f32[5,256,512]{2,1,0:T(8,128)} reshape(f32[5,64,4,512]{3,2,1,0:T(4,128)} %bitcast.83) | data formatting | bytes 5242880 | tf_op jit(solution)/shard_map/reshape | solution.py:167
  122.1 26.8 %shard_map.92 = f32[5,256,512]{2,1,0:T(8,128)} custom-call(f32[5,256,512]{2,1,0:T(8,128)} %reshape.113.rhs_ref, bf16[5,256,512]{2,1,0:T(8,128)(2,1)} %bitcast.90, bf16[5,256,512]{2,1,0:T(8,128)(2,1)} %bitcast.91, bf16[25,256,512]{2,1,0:T(8,128)(2,1)} %bitcast.88), custom_call_target="tpu_custom_call" | custom-call | tf_op jit(solution)/shard_map/pallas_call | solution.py:71
  148.9 3.9 %reshape.114 = f32[5,64,4,512]{3,2,1,0:T(4,128)} reshape(f32[5,256,512]{2,1,0:T(8,128)} %shard_map.92) | data formatting | bytes 5242880 | tf_op jit(solution)/shard_map/reshape | solution.py:159
  152.9 3.7 %copy.77 = f32[5,64,4,512]{3,2,0,1:T(4,128)} copy(f32[5,64,4,512]{3,2,1,0:T(4,128)} %reshape.114) | data formatting | bytes 5242880 | tf_op jit(solution)/shard_map/reshape | solution.py:159
  156.6 4.1 %reshape.115.x_ref = f32[64,80,128]{2,1,0:T(8,128)} reshape(f32[64,5,4,512]{3,2,1,0:T(4,128)} %bitcast.84) | data formatting | bytes 5242880 | tf_op jit(solution)/shard_map/reshape | solution.py:160
  160.7 71.1 %shard_map.93 = f32[64,80,128]{2,1,0:T(8,128)} custom-call(f32[64,80,128]{2,1,0:T(8,128)} %reshape.115.x_ref), custom_call_target="tpu_custom_call" | custom-call | tf_op jit(solution)/shard_map/pallas_call | solution.py:142
  231.8 4.0 %reshape.116 = f32[64,5,4,512]{3,2,1,0:T(4,128)} reshape(f32[64,80,128]{2,1,0:T(8,128)} %shard_map.93) | data formatting | bytes 5242880 | tf_op jit(solution)/shard_map/reshape | solution.py:166
  235.8 5.0 %copy.65 = f32[5,64,4,512]{3,0,2,1:T(8,128)} copy(f32[5,64,4,512]{3,2,0,1:T(4,128)} %bitcast.85) | data formatting | bytes 5242880 | tf_op jit(solution)/shard_map/reshape | solution.py:167
  240.8 2.9 %gather_fusion.1 = f32[128,5,512]{2,1,0:T(8,128)S(1)} fusion(f32[5,256,512]{2,0,1:T(8,128)} %bitcast.87, s32[1024]{0:T(1024)S(1)} %get-tuple-element.50), kind=kCustom, calls=%fused_computation.1 | custom fusion | bytes 2621952 | tf_op jit(solution)/shard_map/jit(_take)/gather | solution.py:214
  243.7 2.1 fusion.1
  (26 shorter events, 0.2 us)
Async XLA Ops:
  0.8 13.0 %collective-permute-start.1 = (f32[5,1,4,512]{3,2,1,0:T(4,128)S(1)}, f32[5,1,4,512]{3,2,1,0:T(4,128)S(1)}, u32[]{:S(2)}, u32[]{:S(2)}) collective-permute-start(f32[5,1,4,512]{3,2,1,0:T(4,128)S(1)} %get-tuple-element.45), channel_id=1, source_target_pairs={{0,4},{4,8},{8,12},{12,16},{16,20},{20,24},{24,28},{28,32},{32,36}... | collective-permute-start | bytes 122888 | tf_op jit(solution)/shard_map/ppermute | solution.py:18
  2.7 8.1 %copy-start.3 = (f32[4,5,5]{2,0,1:T(4,128)S(1)}, f32[4,5,5]{2,0,1:T(4,128)}, u32[]{:S(2)}) copy-start(f32[4,5,5]{2,0,1:T(4,128)} %param.14) | copy-start | bytes 1204
  2.7 8.6 %copy-start.4 = (s32[1,32,4,1]{1,3,2,0:T(1,128)S(1)}, s32[1,32,4,1]{1,3,2,0:T(1,128)}, u32[]{:S(2)}) copy-start(s32[1,32,4,1]{1,3,2,0:T(1,128)} %param.13) | copy-start | bytes 1540
  2.7 10.5 %copy-start.5 = (s32[32,4]{0,1:T(4,128)S(1)}, s32[32,4]{0,1:T(4,128)}, u32[]{:S(2)}) copy-start(s32[32,4]{0,1:T(4,128)} %param.12) | copy-start | bytes 1540
  2.7 11.1 %copy-start = (f32[5,32,4,512]{3,2,1,0:T(4,128)S(1)}, f32[5,32,4,512]{3,2,1,0:T(4,128)}, u32[]{:S(2)}) copy-start(f32[5,32,4,512]{3,2,1,0:T(4,128)} %param.9) | copy-start | bytes 3932164
  2.7 11.6 %collective-permute-start = (f32[5,1,4,512]{3,2,1,0:T(4,128)S(1)}, f32[5,1,4,512]{3,2,1,0:T(4,128)S(1)}, u32[]{:S(2)}, u32[]{:S(2)}) collective-permute-start(f32[5,1,4,512]{3,2,1,0:T(4,128)S(1)} %get-tuple-element.44), channel_id=1, source_target_pairs={{4,0},{8,4},{12,8},{16,12},{20,16},{24,20},{28,24},{32,28},{36,32}... | collective-permute-start | bytes 122888 | tf_op jit(solution)/shard_map/ppermute | solution.py:21
  5.4 10.7 %collective-permute-start.2 = (f32[5,32,1,512]{3,1,2,0:T(8,128)S(1)}, f32[5,32,1,512]{3,1,2,0:T(8,128)S(1)}, u32[]{:S(2)}, u32[]{:S(2)}) collective-permute-start(f32[5,32,1,512]{3,1,2,0:T(8,128)S(1)} %copy.67), channel_id=1, source_target_pairs={{1,0},{2,1},{3,2},{5,4},{6,5},{7,6},{9,8},{10,9},{11,10},{13,12},{... | collective-permute-start | bytes 983048 | tf_op jit(solution)/shard_map/ppermute | solution.py:21
  6.7 10.5 %collective-permute-start.3 = (f32[5,32,1,512]{3,1,2,0:T(8,128)S(1)}, f32[5,32,1,512]{3,1,2,0:T(8,128)S(1)}, u32[]{:S(2)}, u32[]{:S(2)}) collective-permute-start(f32[5,32,1,512]{3,1,2,0:T(8,128)S(1)} %copy.68), channel_id=1, source_target_pairs={{0,1},{1,2},{2,3},{4,5},{5,6},{6,7},{8,9},{9,10},{10,11},{12,13},{... | collective-permute-start | bytes 983048 | tf_op jit(solution)/shard_map/ppermute | solution.py:18
  17.6 1.3 copy-start.1
  17.6 1.3 copy-start.2

commit v3 on v2

--- a/solution.py
+++ b/solution.py
@@ -85,8 +85,8 @@
 MESH = pl.DeviceIdType.MESH
 
 
-def exchange_kernel(x_ref, o_ref, send_sems, recv_sems, local_sem):
-    peers = x_ref.shape[0]
+def exchange_kernel(peers, x_ref, o_ref, send_sems, recv_sems, local_sem):
+    width = x_ref.shape[1] // peers
     me = lax.axis_index("circ")
     plane = lax.axis_index("ax")
     barrier = pltpu.get_barrier_semaphore()
@@ -98,14 +98,15 @@
 
     lax.fori_loop(1, peers, greet, 0)
     pl.semaphore_wait(barrier, peers - 1)
-    local = pltpu.make_async_copy(x_ref.at[me], o_ref.at[me], local_sem)
+    own = pl.ds(me * width, width)
+    local = pltpu.make_async_copy(x_ref.at[:, own], o_ref.at[:, own], local_sem)
     local.start()
 
     def outgoing(i):
         peer = lax.rem(me + i, peers)
         return pltpu.make_async_remote_copy(
-            src_ref=x_ref.at[peer],
-            dst_ref=o_ref.at[me],
+            src_ref=x_ref.at[:, pl.ds(peer * width, width)],
+            dst_ref=o_ref.at[:, pl.ds(me * width, width)],
             send_sem=send_sems.at[peer],
             recv_sem=recv_sems.at[me],
             device_id=(peer, plane),
@@ -115,8 +116,8 @@
     def incoming(i):
         peer = lax.rem(me + peers - i, peers)
         return pltpu.make_async_remote_copy(
-            src_ref=x_ref.at[me],
-            dst_ref=o_ref.at[peer],
+            src_ref=x_ref.at[:, pl.ds(me * width, width)],
+            dst_ref=o_ref.at[:, pl.ds(peer * width, width)],
             send_sem=send_sems.at[me],
             recv_sem=recv_sems.at[peer],
             device_id=(peer, plane),
@@ -137,10 +138,9 @@
     lax.fori_loop(1, peers, finish, 0)
 
 
-def exchange(chunks, collective_id):
-    peers = chunks.shape[0]
+def exchange(chunks, peers, collective_id):
     return pl.pallas_call(
-        exchange_kernel,
+        functools.partial(exchange_kernel, peers),
         out_shape=jax.ShapeDtypeStruct(chunks.shape, chunks.dtype),
         in_specs=[pl.BlockSpec(memory_space=pl.ANY)],
         out_specs=pl.BlockSpec(memory_space=pl.ANY),
@@ -151,20 +151,6 @@
         ],
         compiler_params=pltpu.CompilerParams(collective_id=collective_id, has_side_effects=True),
     )(chunks)
-
-
-def to_chunks(rows, peers):
-    fields, slots, points = rows.shape
-    per_peer = slots // peers
-    flat = rows.reshape(fields, peers, per_peer, points).transpose(1, 0, 2, 3)
-    return flat.reshape(peers, fields * per_peer * points // 128, 128)
-
-
-def from_chunks(chunks, fields, points):
-    peers = chunks.shape[0]
-    per_peer = chunks.shape[1] * 128 // (fields * points)
-    rows = chunks.reshape(peers, fields, per_peer, points).transpose(1, 0, 2, 3)
-    return rows.reshape(fields, peers * per_peer, points)
 
 
 def per_device(
@@ -203,14 +189,14 @@
         [line_rhs, jnp.full((fields, 1, points), jnp.nan, jnp.float32)], axis=1
     )
     outgoing = jnp.take(padded_rhs, line_of_slot, axis=1)
-    owned_rhs = from_chunks(exchange(to_chunks(outgoing, circ_devices), 0), fields, points)
+    owned_rhs = exchange(outgoing, circ_devices, 0)
     owned_solution = line_solve(
         owned_rhs,
         lower_coef[0].transpose(1, 0, 2),
         upper_coef[0].transpose(1, 0, 2),
         pivot_inverse[0].transpose(1, 0, 2),
     )
-    returned = from_chunks(exchange(to_chunks(owned_solution, circ_devices), 1), fields, points)
+    returned = exchange(owned_solution, circ_devices, 1)
     correction = jnp.take(returned, slot_ids, axis=1)
     return adjoint + correction.reshape(fields, circ_cells, axial_cells, points)
 

time: 249 us -> 216 us (0.87)
  local copies, waits for them, and re-layouts: 54.2 us -> 20.5 us
    reshape x9 -> x0, local copies, waits for them, and re-layouts: 36.7 us -> none  [the longest x3 11.8 us: from_chunks(): rows = chunks.reshape(peers, fields, per_peer, points).transpose(1, 0, 2, 3)]
    select_n x1 -> x2, other arithmetic: 0.01 us -> 5.41 us  [per_device(): outgoing = jnp.take(padded_rhs, line_of_slot, axis=1)]
    pallas_call x0 -> x1, local copies, waits for them, and re-layouts: none -> 5.29 us  [exchange(): pl.pallas_call(functools.partial(exchange_kernel, peers), out_shape=jax.S...]
    transpose x1 -> x0, other arithmetic: 4.23 us -> none  [to_chunks(): flat = rows.reshape(fields, peers, per_peer, points).transpose(1, 0, 2, 3)]
  transfers between devices with their start and end apart: 4 -> 4, of which waited for: 1 -> 1; matrix products, arithmetic and copies ran while one was open for 3% -> 4% of each run, Pallas kernels for 0% -> 0%
where the time goes in v3:
time: 216 us; the launch traced here: 214 us
  Pallas kernels  170 us (79%)
  local copies, waits for them, and re-layouts  20.5 us (9%)
  other arithmetic  14.2 us (7%)
  starting transfers between devices  7.24 us (3%)
    pallas_call x2, Pallas kernels, exchange(): pl.pallas_call(functools.partial(exchange_kernel, peers), out_shape=jax.S...  143 us
    pallas_call x1, Pallas kernels, line_solve(): pl.pallas_call(solve_kernel, out_shape=jax.ShapeDtypeStruct(rhs.shape, jn...  26.9 us
    ppermute x2, starting transfers between devices, extended(): lax.ppermute(lax.slice_in_dim(block, block.shape[dim] - width, None, axis...  5.86 us
    select_n x2, other arithmetic, per_device(): outgoing = jnp.take(padded_rhs, line_of_slot, axis=1)  5.41 us
    pallas_call x1, local copies, waits for them, and re-layouts, exchange(): pl.pallas_call(functools.partial(exchange_kernel, peers), out_shape=jax.S...  5.29 us
    select_n x1, other arithmetic, per_device(): residual = jnp.where(active, residual, jnp.nan)  5 us
  transfers between devices with their start and end apart: 4, of which 1 were waited for; matrix products, arithmetic and copies ran while one was open for 4% of the time, Pallas kernels for 0%

profile of v3, /device:TPU:25, one launch (start us, length us, event | category | flops | bytes accessed | tf_op | source)
XLA Modules:
  0.0 213.9 jit_solution(5256059260657935850)
XLA Ops:
  0.0 0.8 fusion.8
  0.8 1.9 collective-permute-start.1
  2.7 0.1 collective-permute-start
  2.8 2.6 %fusion.9 = (f32[5,32,1,512]{3,2,1,0:T(1,128)S(1)}, f32[5,32,1,512]{3,2,1,0:T(1,128)S(1)}) fusion(f32[5,32,4,512]{3,2,1,0:T(4,128)} %param.9), kind=kLoop, calls=%fused_computation.71 | loop fusion | bytes 1310720 | tf_op jit(solution)/shard_map/slice | solution.py:21
  5.4 1.3 collective-permute-start.2
  6.7 4.0 %collective-permute-start.3 = (f32[5,32,1,512]{3,1,2,0:T(8,128)S(1)}, f32[5,32,1,512]{3,1,2,0:T(8,128)S(1)}, u32[]{:S(2)}, u32[]{:S(2)}) collective-permute-start(f32[5,32,1,512]{3,1,2,0:T(8,128)S(1)} %copy.51), channel_id=1, source_target_pairs={{0,1},{1,2},{2,3},{4,5},{5,6},{6,7},{8,9},{9,10},{10,11},{12,13},{... | collective-permute-start | bytes 983048 | tf_op jit(solution)/shard_map/ppermute | solution.py:18
  10.7 0.0 copy-done.3
  10.7 0.4 slice_reduce_fusion.19
  11.1 0.2 slice_reduce_fusion.1
  11.3 0.0 copy-done.4
  11.3 0.1 copy.37
  11.4 0.1 copy.40
  11.5 0.1 mul.373
  11.6 0.1 reshape.84
  11.7 0.2 convert_reduce_fusion
  11.9 1.2 scatter_custom_fusion
  13.1 0.1 reduce_sum.14
  13.2 0.0 copy-done.5
  13.2 0.1 copy.41
  13.3 0.1 iota_compare_fusion
  13.4 0.1 copy.38
  13.5 0.1 copy.39
  13.6 0.0 collective-permute-done.1
  13.7 0.5 constant_dynamic-update-slice_fusion.1
  14.2 0.0 collective-permute-done
  14.2 0.2 slice_bitcast_fusion.9
  14.5 0.2 slice_bitcast_fusion.4
  14.7 1.4 collective-permute-done.2
  16.1 0.3 copy.43
  16.5 0.8 maximum_bitcast_fusion.7
  17.2 0.0 collective-permute-done.3
  17.2 0.3 copy.45
  17.6 0.0 copy-start.1
  17.6 0.0 copy-start.2
  17.6 0.6 maximum_bitcast_fusion.3
  18.2 0.7 copy-done.1
  18.9 0.0 copy-done.2
  18.9 5.0 %add_select_fusion = f32[5,32,4,512]{3,2,1,0:T(4,128)S(1)} fusion(f32[5,32,4,512]{3,2,1,0:T(4,128)S(1)} %copy-done.1, f32[5,32,4,512]{3,2,1,0:T(4,128)S(1)} %copy-done, f32[32,4,512]{2,1,0:T(4,128)S(1)} %get-tuple-element.32, f32[5]{0:T(128)S(1)} %get-tuple-element.23, f32[32,4,512]{2,1,0:T(4,128)S(1)} %get-tuple-element.33, f32[5]{0:T(128)S(1)} %slice_reduce_fusion.1, ...), kind=kLoop, calls=%fused_computation.7 | loop fusion | flops 14090240 | bytes 9503120 | tf_op jit(solution)/shard_map/jit(_where)/select_n | solution.py:179
  23.9 0.8 copy.46
  24.7 0.2 concatenate.21
  25.0 3.0 %gather_fusion = f32[256,5,512]{2,1,0:T(8,128)} fusion(f32[5,129,512]{2,0,1:T(8,128)S(1)} %concatenate.21, s32[1024]{0:T(1024)S(1)} %get-tuple-element.51), kind=kCustom, calls=%fused_computation | custom fusion | bytes 5243904 | tf_op jit(solution)/shard_map/jit(_take)/gather | solution.py:191
  28.0 5.4 %fusion.x_ref = f32[5,256,512]{2,1,0:T(8,128)} fusion(f32[256,5,512]{2,1,0:T(8,128)} %gather_fusion, pred[256]{0:T(512)(128)(4,1)S(1)} %compare_and_fusion), kind=kLoop, calls=%fused_computation.4 | loop fusion | flops 655360 | bytes 5243136 | tf_op jit(solution)/shard_map/jit(_take)/select_n | solution.py:191
  33.4 71.6 %shard_map.91.rhs_ref = f32[5,256,512]{2,1,0:T(8,128)} custom-call(f32[5,256,512]{2,1,0:T(8,128)} %fusion.x_ref), custom_call_target="tpu_custom_call" | custom-call | tf_op jit(solution)/shard_map/pallas_call | solution.py:142
  105.0 26.9 %shard_map.92.x_ref = f32[5,256,512]{2,1,0:T(8,128)} custom-call(f32[5,256,512]{2,1,0:T(8,128)} %shard_map.91.rhs_ref, bf16[5,256,512]{2,1,0:T(8,128)(2,1)} %bitcast.73, bf16[5,256,512]{2,1,0:T(8,128)(2,1)} %bitcast.74, bf16[25,256,512]{2,1,0:T(8,128)(2,1)} %bitcast.71), custom_call_target="tpu_custom_call" | custom-call | tf_op jit(solution)/shard_map/pallas_call | solution.py:71
  131.9 71.8 %shard_map.93 = f32[5,256,512]{2,1,0:T(8,128)} custom-call(f32[5,256,512]{2,1,0:T(8,128)} %shard_map.92.x_ref), custom_call_target="tpu_custom_call" | custom-call | tf_op jit(solution)/shard_map/pallas_call | solution.py:142
  203.7 5.3 %copy.48 = f32[5,256,512]{2,0,1:T(8,128)} copy(f32[5,256,512]{2,1,0:T(8,128)} %shard_map.93) | data formatting | bytes 5242880 | tf_op jit(solution)/shard_map/pallas_call | solution.py:142
  209.0 2.9 %gather_fusion.1 = f32[128,5,512]{2,1,0:T(8,128)S(1)} fusion(f32[5,256,512]{2,0,1:T(8,128)} %copy.48, s32[1024]{0:T(1024)S(1)} %get-tuple-element.50), kind=kCustom, calls=%fused_computation.1 | custom fusion | bytes 2621952 | tf_op jit(solution)/shard_map/jit(_take)/gather | solution.py:200
  211.8 2.1 fusion.1
  (16 shorter events, 0.1 us)
Async XLA Ops:
  0.8 12.8 %collective-permute-start.1 = (f32[5,1,4,512]{3,2,1,0:T(4,128)S(1)}, f32[5,1,4,512]{3,2,1,0:T(4,128)S(1)}, u32[]{:S(2)}, u32[]{:S(2)}) collective-permute-start(f32[5,1,4,512]{3,2,1,0:T(4,128)S(1)} %get-tuple-element.45), channel_id=1, source_target_pairs={{0,4},{4,8},{8,12},{12,16},{16,20},{20,24},{24,28},{28,32},{32,36}... | collective-permute-start | bytes 122888 | tf_op jit(solution)/shard_map/ppermute | solution.py:18
  2.7 8.1 %copy-start.3 = (f32[4,5,5]{2,0,1:T(4,128)S(1)}, f32[4,5,5]{2,0,1:T(4,128)}, u32[]{:S(2)}) copy-start(f32[4,5,5]{2,0,1:T(4,128)} %param.14) | copy-start | bytes 1204
  2.7 8.6 %copy-start.4 = (s32[1,32,4,1]{1,3,2,0:T(1,128)S(1)}, s32[1,32,4,1]{1,3,2,0:T(1,128)}, u32[]{:S(2)}) copy-start(s32[1,32,4,1]{1,3,2,0:T(1,128)} %param.13) | copy-start | bytes 1540
  2.7 10.5 %copy-start.5 = (s32[32,4]{0,1:T(4,128)S(1)}, s32[32,4]{0,1:T(4,128)}, u32[]{:S(2)}) copy-start(s32[32,4]{0,1:T(4,128)} %param.12) | copy-start | bytes 1540
  2.7 11.0 %copy-start = (f32[5,32,4,512]{3,2,1,0:T(4,128)S(1)}, f32[5,32,4,512]{3,2,1,0:T(4,128)}, u32[]{:S(2)}) copy-start(f32[5,32,4,512]{3,2,1,0:T(4,128)} %param.9) | copy-start | bytes 3932164
  2.7 11.5 %collective-permute-start = (f32[5,1,4,512]{3,2,1,0:T(4,128)S(1)}, f32[5,1,4,512]{3,2,1,0:T(4,128)S(1)}, u32[]{:S(2)}, u32[]{:S(2)}) collective-permute-start(f32[5,1,4,512]{3,2,1,0:T(4,128)S(1)} %get-tuple-element.44), channel_id=1, source_target_pairs={{4,0},{8,4},{12,8},{16,12},{20,16},{24,20},{28,24},{32,28},{36,32}... | collective-permute-start | bytes 122888 | tf_op jit(solution)/shard_map/ppermute | solution.py:21
  5.4 10.7 %collective-permute-start.2 = (f32[5,32,1,512]{3,1,2,0:T(8,128)S(1)}, f32[5,32,1,512]{3,1,2,0:T(8,128)S(1)}, u32[]{:S(2)}, u32[]{:S(2)}) collective-permute-start(f32[5,32,1,512]{3,1,2,0:T(8,128)S(1)} %copy.50), channel_id=1, source_target_pairs={{1,0},{2,1},{3,2},{5,4},{6,5},{7,6},{9,8},{10,9},{11,10},{13,12},{... | collective-permute-start | bytes 983048 | tf_op jit(solution)/shard_map/ppermute | solution.py:21
  6.7 10.5 %collective-permute-start.3 = (f32[5,32,1,512]{3,1,2,0:T(8,128)S(1)}, f32[5,32,1,512]{3,1,2,0:T(8,128)S(1)}, u32[]{:S(2)}, u32[]{:S(2)}) collective-permute-start(f32[5,32,1,512]{3,1,2,0:T(8,128)S(1)} %copy.51), channel_id=1, source_target_pairs={{0,1},{1,2},{2,3},{4,5},{5,6},{6,7},{8,9},{9,10},{10,11},{12,13},{... | collective-permute-start | bytes 983048 | tf_op jit(solution)/shard_map/ppermute | solution.py:18
  17.6 1.3 copy-start.1
  17.6 1.3 copy-start.2

commit v4 on v3

--- a/solution.py
+++ b/solution.py
@@ -45,43 +45,6 @@
     return value
 
 
-def solve_kernel(rhs_ref, lower_ref, upper_ref, pivot_ref, out_ref):
-    fields, rows, points = rhs_ref.shape
-    pos = lax.broadcasted_iota(jnp.int32, (fields, rows, points), 2)
-    rhs = rhs_ref[...]
-    active = rhs == rhs
-    forward_coef = jnp.where(active, -lower_ref[...].astype(jnp.float32), 0.0)
-    interim = scan_forward(forward_coef, jnp.where(active, rhs, 0.0), pos)
-    applied = []
-    for f in range(fields):
-        total = pivot_ref[f * fields].astype(jnp.float32) * interim[0]
-        for g in range(1, fields):
-            total = total + pivot_ref[f * fields + g].astype(jnp.float32) * interim[g]
-        applied.append(total)
-    applied = jnp.stack(applied, axis=0)
-    backward_coef = jnp.where(active, -upper_ref[...].astype(jnp.float32), 0.0)
-    out_ref[...] = scan_backward(backward_coef, jnp.where(active, applied, 0.0), pos)
-
-
-def line_solve(rhs, lower, upper, pivot, block_rows=16):
-    fields, lines, points = rhs.shape
-    blocks = pivot.shape[0]
-    grid = (lines // block_rows,)
-    field_spec = pl.BlockSpec((fields, block_rows, points), lambda i: (0, i, 0))
-    return pl.pallas_call(
-        solve_kernel,
-        out_shape=jax.ShapeDtypeStruct(rhs.shape, jnp.float32),
-        grid=grid,
-        in_specs=[
-            field_spec,
-            field_spec,
-            field_spec,
-            pl.BlockSpec((blocks, block_rows, points), lambda i: (0, i, 0)),
-        ],
-        out_specs=field_spec,
-    )(rhs, lower, upper, pivot)
-
-
 MESH = pl.DeviceIdType.MESH
 
 
@@ -151,6 +114,161 @@
         ],
         compiler_params=pltpu.CompilerParams(collective_id=collective_id, has_side_effects=True),
     )(chunks)
+
+
+def solve_rows(rhs, lower, upper, pivot):
+    fields, rows, points = rhs.shape
+    pos = lax.broadcasted_iota(jnp.int32, (fields, rows, points), 2)
+    active = rhs == rhs
+    forward_coef = jnp.where(active, -lower.astype(jnp.float32), 0.0)
+    interim = scan_forward(forward_coef, jnp.where(active, rhs, 0.0), pos)
+    applied = []
+    for f in range(fields):
+        total = pivot[f * fields].astype(jnp.float32) * interim[0]
+        for g in range(1, fields):
+            total = total + pivot[f * fields + g].astype(jnp.float32) * interim[g]
+        applied.append(total)
+    applied = jnp.stack(applied, axis=0)
+    backward_coef = jnp.where(active, -upper.astype(jnp.float32), 0.0)
+    return scan_backward(backward_coef, jnp.where(active, applied, 0.0), pos)
+
+
+def owner_kernel(
+    peers, group, rhs_ref, lower_ref, upper_ref, pivot_ref, out_ref,
+    rhs_in, solved, lower_v, upper_v, pivot_v,
+    send_rhs, recv_rhs, send_sol, recv_sol, local_sems,
+):
+    width = rhs_ref.shape[1] // peers
+    groups = peers // group
+    rows = group * width
+    me = lax.axis_index("circ")
+    plane = lax.axis_index("ax")
+    mine = me // group
+    factor_copies = [
+        pltpu.make_async_copy(lower_ref, lower_v, local_sems.at[0]),
+        pltpu.make_async_copy(upper_ref, upper_v, local_sems.at[1]),
+        pltpu.make_async_copy(pivot_ref, pivot_v, local_sems.at[2]),
+    ]
+    for copy in factor_copies:
+        copy.start()
+    barrier = pltpu.get_barrier_semaphore()
+
+    def greet(i, carry):
+        peer = lax.rem(me + i, peers)
+        pl.semaphore_signal(barrier, inc=1, device_id=(peer, plane), device_id_type=MESH)
+        return carry
+
+    lax.fori_loop(1, peers, greet, 0)
+    pl.semaphore_wait(barrier, peers - 1)
+
+    def window(index):
+        return pl.ds(index * width, width)
+
+    def rhs_copy(source, target):
+        return pltpu.make_async_remote_copy(
+            src_ref=rhs_ref.at[:, window(target)],
+            dst_ref=rhs_in.at[:, window(source)],
+            send_sem=send_rhs.at[target],
+            recv_sem=recv_rhs.at[source],
+            device_id=(lax.select(source == me, target, source), plane),
+            device_id_type=MESH,
+        )
+
+    def sol_copy(source, target):
+        return pltpu.make_async_remote_copy(
+            src_ref=solved.at[:, window(target)],
+            dst_ref=out_ref.at[:, window(source)],
+            send_sem=send_sol.at[target],
+            recv_sem=recv_sol.at[source],
+            device_id=(lax.select(source == me, target, source), plane),
+            device_id_type=MESH,
+        )
+
+    own_rhs = pltpu.make_async_copy(rhs_ref.at[:, window(me)], rhs_in.at[:, window(me)], local_sems.at[3])
+    own_sol = pltpu.make_async_copy(solved.at[:, window(me)], out_ref.at[:, window(me)], local_sems.at[4])
+
+    def send(i, carry):
+        target = group * lax.rem(mine - i // group + groups, groups) + i % group
+
+        @pl.when(target == me)
+        def _():
+            own_rhs.start()
+
+        @pl.when(target != me)
+        def _():
+            rhs_copy(me, target).start()
+
+        return carry
+
+    lax.fori_loop(0, peers, send, 0)
+    for copy in factor_copies:
+        copy.wait()
+
+    def solve(j, carry):
+        g = lax.rem(mine + j, groups)
+        for r in range(group):
+            source = g * group + r
+
+            @pl.when(source == me)
+            def _():
+                own_rhs.wait()
+
+            @pl.when(source != me)
+            def _():
+                rhs_copy(source, me).wait_recv()
+
+        block = pl.ds(pl.multiple_of(g * rows, rows), rows)
+        solved[:, block, :] = solve_rows(
+            rhs_in[:, block, :], lower_v[:, block, :], upper_v[:, block, :], pivot_v[:, block, :]
+        )
+        for r in range(group):
+            target = g * group + r
+
+            @pl.when(target == me)
+            def _():
+                own_sol.start()
+
+            @pl.when(target != me)
+            def _():
+                sol_copy(me, target).start()
+
+        return carry
+
+    lax.fori_loop(0, groups, solve, 0)
+
+    def finish(i, carry):
+        peer = lax.rem(me + i, peers)
+        rhs_copy(me, peer).wait_send()
+        sol_copy(me, peer).wait_send()
+        sol_copy(peer, me).wait_recv()
+        return carry
+
+    lax.fori_loop(1, peers, finish, 0)
+    own_sol.wait()
+
+
+def owner_solve(rhs, lower, upper, pivot, peers, group=4):
+    return pl.pallas_call(
+        functools.partial(owner_kernel, peers, group),
+        out_shape=jax.ShapeDtypeStruct(rhs.shape, rhs.dtype),
+        in_specs=[pl.BlockSpec(memory_space=pl.ANY)] * 4,
+        out_specs=pl.BlockSpec(memory_space=pl.ANY),
+        scratch_shapes=[
+            pltpu.VMEM(rhs.shape, jnp.float32),
+            pltpu.VMEM(rhs.shape, jnp.float32),
+            pltpu.VMEM(lower.shape, lower.dtype),
+            pltpu.VMEM(upper.shape, upper.dtype),
+            pltpu.VMEM(pivot.shape, pivot.dtype),
+            pltpu.SemaphoreType.DMA((peers,)),
+            pltpu.SemaphoreType.DMA((peers,)),
+            pltpu.SemaphoreType.DMA((peers,)),
+            pltpu.SemaphoreType.DMA((peers,)),
+            pltpu.SemaphoreType.DMA((5,)),
+        ],
+        compiler_params=pltpu.CompilerParams(
+            collective_id=0, has_side_effects=True, vmem_limit_bytes=48 * 1024 * 1024
+        ),
+    )(rhs, lower, upper, pivot)
 
 
 def per_device(
@@ -189,14 +307,13 @@
         [line_rhs, jnp.full((fields, 1, points), jnp.nan, jnp.float32)], axis=1
     )
     outgoing = jnp.take(padded_rhs, line_of_slot, axis=1)
-    owned_rhs = exchange(outgoing, circ_devices, 0)
-    owned_solution = line_solve(
-        owned_rhs,
+    returned = owner_solve(
+        outgoing,
         lower_coef[0].transpose(1, 0, 2),
         upper_coef[0].transpose(1, 0, 2),
         pivot_inverse[0].transpose(1, 0, 2),
-    )
-    returned = exchange(owned_solution, circ_devices, 1)
+        circ_devices,
+    )
     correction = jnp.take(returned, slot_ids, axis=1)
     return adjoint + correction.reshape(fields, circ_cells, axial_cells, points)
 

time: 216 us -> 181 us (0.84)
  Pallas kernels: 170 us -> 136 us
    pallas_call x3 -> x1, Pallas kernels: 170 us -> 136 us  [owner_solve(): pl.pallas_call(functools.partial(owner_kernel, peers, group), out_shape=j...]
where the time goes in v4:
time: 181 us; the launch traced here: 178 us
  Pallas kernels  136 us (75%)
  local copies, waits for them, and re-layouts  18.8 us (10%)
  other arithmetic  14.4 us (8%)
  starting transfers between devices  7.24 us (4%)
    pallas_call x1, Pallas kernels, owner_solve(): pl.pallas_call(functools.partial(owner_kernel, peers, group), out_shape=j...  136 us
    ppermute x2, starting transfers between devices, extended(): lax.ppermute(lax.slice_in_dim(block, block.shape[dim] - width, None, axis...  5.86 us
    select_n x2, other arithmetic, per_device(): outgoing = jnp.take(padded_rhs, line_of_slot, axis=1)  5.56 us
    select_n x1, other arithmetic, per_device(): residual = jnp.where(active, residual, jnp.nan)  5 us
  transfers between devices with their start and end apart: 4, of which 1 were waited for; matrix products, arithmetic and copies ran while one was open for 4% of the time, Pallas kernels for 0%

profile of v4, /device:TPU:25, one launch (start us, length us, event | category | flops | bytes accessed | tf_op | source)
XLA Modules:
  0.0 178.1 jit_solution(4090590777503154180)
XLA Ops:
  0.0 0.8 fusion.8
  0.8 1.9 %collective-permute-start.1 = (f32[5,1,4,512]{3,2,1,0:T(4,128)S(1)}, f32[5,1,4,512]{3,2,1,0:T(4,128)S(1)}, u32[]{:S(2)}, u32[]{:S(2)}) collective-permute-start(f32[5,1,4,512]{3,2,1,0:T(4,128)S(1)} %get-tuple-element.45), channel_id=1, source_target_pairs={{0,4},{4,8},{8,12},{12,16},{16,20},{20,24},{24,28},{28,32},{32,36}... | collective-permute-start | bytes 122888 | tf_op jit(solution)/shard_map/ppermute | solution.py:18
  2.7 0.1 collective-permute-start
  2.8 2.6 %fusion.9 = (f32[5,32,1,512]{3,2,1,0:T(1,128)S(1)}, f32[5,32,1,512]{3,2,1,0:T(1,128)S(1)}) fusion(f32[5,32,4,512]{3,2,1,0:T(4,128)} %param.9), kind=kLoop, calls=%fused_computation.71 | loop fusion | bytes 1310720 | tf_op jit(solution)/shard_map/slice | solution.py:21
  5.4 1.3 collective-permute-start.2
  6.7 4.0 %collective-permute-start.3 = (f32[5,32,1,512]{3,1,2,0:T(8,128)S(1)}, f32[5,32,1,512]{3,1,2,0:T(8,128)S(1)}, u32[]{:S(2)}, u32[]{:S(2)}) collective-permute-start(f32[5,32,1,512]{3,1,2,0:T(8,128)S(1)} %copy.51), channel_id=1, source_target_pairs={{0,1},{1,2},{2,3},{4,5},{5,6},{6,7},{8,9},{9,10},{10,11},{12,13},{... | collective-permute-start | bytes 983048 | tf_op jit(solution)/shard_map/ppermute | solution.py:18
  10.7 0.0 copy-done.5
  10.7 0.4 slice_reduce_fusion.19
  11.1 0.2 slice_reduce_fusion.1
  11.3 0.0 copy-done.6
  11.3 0.1 copy.37
  11.4 0.1 copy.40
  11.5 0.1 mul.373
  11.6 0.1 reshape.84
  11.7 0.2 convert_reduce_fusion
  11.9 1.2 scatter_custom_fusion
  13.1 0.1 reduce_sum.14
  13.2 0.0 copy-done.7
  13.2 0.1 copy.41
  13.3 0.1 iota_compare_fusion
  13.4 0.1 copy.38
  13.5 0.1 copy.39
  13.6 0.0 collective-permute-done.1
  13.7 0.0 copy-done.2
  13.7 0.5 constant_dynamic-update-slice_fusion.1
  14.2 0.0 collective-permute-done
  14.2 0.2 slice_bitcast_fusion.9
  14.5 0.2 slice_bitcast_fusion.4
  14.7 1.4 collective-permute-done.2
  16.1 0.3 copy.43
  16.5 0.8 maximum_bitcast_fusion.7
  17.2 0.0 collective-permute-done.3
  17.2 0.3 copy.45
  17.6 0.0 copy-start.3
  17.6 0.0 copy-start.4
  17.6 0.6 maximum_bitcast_fusion.3
  18.2 0.7 copy-done.3
  18.9 0.0 copy-done.4
  18.9 5.0 %add_select_fusion = f32[5,32,4,512]{3,2,1,0:T(4,128)S(1)} fusion(f32[5,32,4,512]{3,2,1,0:T(4,128)S(1)} %copy-done.3, f32[5,32,4,512]{3,2,1,0:T(4,128)S(1)} %copy-done.2, f32[32,4,512]{2,1,0:T(4,128)S(1)} %get-tuple-element.32, f32[5]{0:T(128)S(1)} %get-tuple-element.23, f32[32,4,512]{2,1,0:T(4,128)S(1)} %get-tuple-element.33, f32[5]{0:T(128)S(1)} %slice_reduce_fusion.1, ...), kind=kLoop, calls=%fused_computation.7 | loop fusion | flops 14090240 | bytes 9503120 | tf_op jit(solution)/shard_map/jit(_where)/select_n | solution.py:297
  23.9 0.8 copy.46
  24.7 0.2 concatenate.21
  25.0 3.0 %gather_fusion = f32[256,5,512]{2,1,0:T(8,128)} fusion(f32[5,129,512]{2,0,1:T(8,128)S(1)} %concatenate.21, s32[1024]{0:T(1024)S(1)} %get-tuple-element.51), kind=kCustom, calls=%fused_computation | custom fusion | bytes 5243904 | tf_op jit(solution)/shard_map/jit(_take)/gather | solution.py:309
  28.0 5.6 %fusion.rhs_ref = f32[5,256,512]{2,1,0:T(8,128)} fusion(f32[256,5,512]{2,1,0:T(8,128)} %gather_fusion, pred[256]{0:T(512)(128)(4,1)S(1)} %compare_and_fusion), kind=kLoop, calls=%fused_computation.4 | loop fusion | flops 655360 | bytes 5243136 | tf_op jit(solution)/shard_map/jit(_take)/select_n | solution.py:309
  33.5 0.0 copy-done
  33.5 136.1 %shard_map.91 = f32[5,256,512]{2,1,0:T(8,128)S(1)} custom-call(f32[5,256,512]{2,1,0:T(8,128)} %fusion.rhs_ref, bf16[5,256,512]{2,1,0:T(8,128)(2,1)S(1)} %bitcast.70, bf16[5,256,512]{2,1,0:T(8,128)(2,1)S(1)} %bitcast.71, bf16[25,256,512]{2,1,0:T(8,128)(2,1)} %bitcast.73), custom_call_target="tpu_custom_call" | custom-call | tf_op jit(solution)/shard_map/pallas_call | solution.py:251
  169.6 3.5 %copy.48 = f32[5,256,512]{2,0,1:T(8,128)} copy(f32[5,256,512]{2,1,0:T(8,128)S(1)} %shard_map.91) | data formatting | bytes 5242880 | tf_op jit(solution)/shard_map/pallas_call | solution.py:251
  173.1 2.9 %gather_fusion.1 = f32[128,5,512]{2,1,0:T(8,128)S(1)} fusion(f32[5,256,512]{2,0,1:T(8,128)} %copy.48, s32[1024]{0:T(1024)S(1)} %get-tuple-element.50), kind=kCustom, calls=%fused_computation.1 | custom fusion | bytes 2621952 | tf_op jit(solution)/shard_map/jit(_take)/gather | solution.py:317
  176.0 2.1 %fusion.1 = f32[5,32,4,512]{3,2,1,0:T(4,128)} fusion(f32[5,32,4,512]{3,2,1,0:T(4,128)S(1)} %copy-done.2, f32[5,32,4,512]{3,0,2,1:T(8,128)S(1)} %bitcast.74, pred[32,4]{1,0:T(8,128)(4,1)S(1)} %copy.39), kind=kLoop, calls=%fused_computation.6 | loop fusion | flops 655360 | bytes 3932288 | tf_op jit(solution)/shard_map/add | solution.py:318
  (18 shorter events, 0.1 us)
Async XLA Ops:
  0.8 12.8 %collective-permute-start.1 = (f32[5,1,4,512]{3,2,1,0:T(4,128)S(1)}, f32[5,1,4,512]{3,2,1,0:T(4,128)S(1)}, u32[]{:S(2)}, u32[]{:S(2)}) collective-permute-start(f32[5,1,4,512]{3,2,1,0:T(4,128)S(1)} %get-tuple-element.45), channel_id=1, source_target_pairs={{0,4},{4,8},{8,12},{12,16},{16,20},{20,24},{24,28},{28,32},{32,36}... | collective-permute-start | bytes 122888 | tf_op jit(solution)/shard_map/ppermute | solution.py:18
  2.7 8.1 %copy-start.5 = (f32[4,5,5]{2,0,1:T(4,128)S(1)}, f32[4,5,5]{2,0,1:T(4,128)}, u32[]{:S(2)}) copy-start(f32[4,5,5]{2,0,1:T(4,128)} %param.14) | copy-start | bytes 1204
  2.7 8.6 %copy-start.6 = (s32[1,32,4,1]{1,3,2,0:T(1,128)S(1)}, s32[1,32,4,1]{1,3,2,0:T(1,128)}, u32[]{:S(2)}) copy-start(s32[1,32,4,1]{1,3,2,0:T(1,128)} %param.13) | copy-start | bytes 1540
  2.7 10.5 %copy-start.7 = (s32[32,4]{0,1:T(4,128)S(1)}, s32[32,4]{0,1:T(4,128)}, u32[]{:S(2)}) copy-start(s32[32,4]{0,1:T(4,128)} %param.12) | copy-start | bytes 1540
  2.7 11.0 %copy-start.2 = (f32[5,32,4,512]{3,2,1,0:T(4,128)S(1)}, f32[5,32,4,512]{3,2,1,0:T(4,128)}, u32[]{:S(2)}) copy-start(f32[5,32,4,512]{3,2,1,0:T(4,128)} %param.9) | copy-start | bytes 3932164
  2.7 11.5 %collective-permute-start = (f32[5,1,4,512]{3,2,1,0:T(4,128)S(1)}, f32[5,1,4,512]{3,2,1,0:T(4,128)S(1)}, u32[]{:S(2)}, u32[]{:S(2)}) collective-permute-start(f32[5,1,4,512]{3,2,1,0:T(4,128)S(1)} %get-tuple-element.44), channel_id=1, source_target_pairs={{4,0},{8,4},{12,8},{16,12},{20,16},{24,20},{28,24},{32,28},{36,32}... | collective-permute-start | bytes 122888 | tf_op jit(solution)/shard_map/ppermute | solution.py:21
  5.4 10.7 %collective-permute-start.2 = (f32[5,32,1,512]{3,1,2,0:T(8,128)S(1)}, f32[5,32,1,512]{3,1,2,0:T(8,128)S(1)}, u32[]{:S(2)}, u32[]{:S(2)}) collective-permute-start(f32[5,32,1,512]{3,1,2,0:T(8,128)S(1)} %copy.50), channel_id=1, source_target_pairs={{1,0},{2,1},{3,2},{5,4},{6,5},{7,6},{9,8},{10,9},{11,10},{13,12},{... | collective-permute-start | bytes 983048 | tf_op jit(solution)/shard_map/ppermute | solution.py:21
  6.7 10.5 %collective-permute-start.3 = (f32[5,32,1,512]{3,1,2,0:T(8,128)S(1)}, f32[5,32,1,512]{3,1,2,0:T(8,128)S(1)}, u32[]{:S(2)}, u32[]{:S(2)}) collective-permute-start(f32[5,32,1,512]{3,1,2,0:T(8,128)S(1)} %copy.51), channel_id=1, source_target_pairs={{0,1},{1,2},{2,3},{4,5},{5,6},{6,7},{8,9},{9,10},{10,11},{12,13},{... | collective-permute-start | bytes 983048 | tf_op jit(solution)/shard_map/ppermute | solution.py:18
  17.6 1.3 copy-start.3
  17.6 1.3 copy-start.4
  28.0 5.6 %copy-start = (bf16[1,256,5,512]{3,1,2,0:T(8,128)(2,1)S(1)}, bf16[1,256,5,512]{3,1,2,0:T(8,128)(2,1)}, u32[]{:S(2)}) copy-start(bf16[1,256,5,512]{3,1,2,0:T(8,128)(2,1)} %param.15) | copy-start | bytes 3932164
  28.0 5.6 %copy-start.1 = (bf16[1,256,5,512]{3,1,2,0:T(8,128)(2,1)S(1)}, bf16[1,256,5,512]{3,1,2,0:T(8,128)(2,1)}, u32[]{:S(2)}) copy-start(bf16[1,256,5,512]{3,1,2,0:T(8,128)(2,1)} %param.16) | copy-start | bytes 3932164

commit v5 on v4

--- a/solution.py
+++ b/solution.py
@@ -138,7 +138,8 @@
     rhs_in, solved, lower_v, upper_v, pivot_v,
     send_rhs, recv_rhs, send_sol, recv_sol, local_sems,
 ):
-    width = rhs_ref.shape[1] // peers
+    width = rhs_ref.shape[0] // peers
+    fields, _, points = lower_ref.shape
     groups = peers // group
     rows = group * width
     me = lax.axis_index("circ")
@@ -166,8 +167,8 @@
 
     def rhs_copy(source, target):
         return pltpu.make_async_remote_copy(
-            src_ref=rhs_ref.at[:, window(target)],
-            dst_ref=rhs_in.at[:, window(source)],
+            src_ref=rhs_ref.at[window(target)],
+            dst_ref=rhs_in.at[window(source)],
             send_sem=send_rhs.at[target],
             recv_sem=recv_rhs.at[source],
             device_id=(lax.select(source == me, target, source), plane),
@@ -176,16 +177,16 @@
 
     def sol_copy(source, target):
         return pltpu.make_async_remote_copy(
-            src_ref=solved.at[:, window(target)],
-            dst_ref=out_ref.at[:, window(source)],
+            src_ref=solved.at[window(target)],
+            dst_ref=out_ref.at[window(source)],
             send_sem=send_sol.at[target],
             recv_sem=recv_sol.at[source],
             device_id=(lax.select(source == me, target, source), plane),
             device_id_type=MESH,
         )
 
-    own_rhs = pltpu.make_async_copy(rhs_ref.at[:, window(me)], rhs_in.at[:, window(me)], local_sems.at[3])
-    own_sol = pltpu.make_async_copy(solved.at[:, window(me)], out_ref.at[:, window(me)], local_sems.at[4])
+    own_rhs = pltpu.make_async_copy(rhs_ref.at[window(me)], rhs_in.at[window(me)], local_sems.at[3])
+    own_sol = pltpu.make_async_copy(solved.at[window(me)], out_ref.at[window(me)], local_sems.at[4])
 
     def send(i, carry):
         target = group * lax.rem(mine - i // group + groups, groups) + i % group
@@ -218,9 +219,11 @@
                 rhs_copy(source, me).wait_recv()
 
         block = pl.ds(pl.multiple_of(g * rows, rows), rows)
-        solved[:, block, :] = solve_rows(
-            rhs_in[:, block, :], lower_v[:, block, :], upper_v[:, block, :], pivot_v[:, block, :]
-        )
+        by_field = [pl.ds(f * points, points) for f in range(fields)]
+        rhs = jnp.stack([rhs_in[block, lanes] for lanes in by_field], axis=0)
+        result = solve_rows(rhs, lower_v[:, block, :], upper_v[:, block, :], pivot_v[:, block, :])
+        for f, lanes in enumerate(by_field):
+            solved[block, lanes] = result[f]
         for r in range(group):
             target = g * group + r
 
@@ -295,7 +298,7 @@
     residual = source - adjoint + step_size[None] * coupled
     active = jnp.arange(points)[None, None, None, :] < lengths[None, :, :, None]
     residual = jnp.where(active, residual, jnp.nan)
-    line_rhs = residual.reshape(fields, line_count, points)
+    line_rhs = residual.transpose(1, 2, 0, 3).reshape(line_count, fields * points)
     targets = line_owner.reshape(line_count)
     ordinal = jnp.arange(line_count)
     earlier_same = (targets[:, None] == targets[None, :]) & (ordinal[None, :] < ordinal[:, None])
@@ -304,9 +307,9 @@
         ordinal.astype(jnp.int32)
     )
     padded_rhs = jnp.concatenate(
-        [line_rhs, jnp.full((fields, 1, points), jnp.nan, jnp.float32)], axis=1
-    )
-    outgoing = jnp.take(padded_rhs, line_of_slot, axis=1)
+        [line_rhs, jnp.full((1, fields * points), jnp.nan, jnp.float32)], axis=0
+    )
+    outgoing = jnp.take(padded_rhs, line_of_slot, axis=0)
     returned = owner_solve(
         outgoing,
         lower_coef[0].transpose(1, 0, 2),
@@ -314,8 +317,9 @@
         pivot_inverse[0].transpose(1, 0, 2),
         circ_devices,
     )
-    correction = jnp.take(returned, slot_ids, axis=1)
-    return adjoint + correction.reshape(fields, circ_cells, axial_cells, points)
+    correction = jnp.take(returned, slot_ids, axis=0)
+    correction = correction.reshape(circ_cells, axial_cells, fields, points).transpose(2, 0, 1, 3)
+    return adjoint + correction
 
 
 def solution(mesh):

time: 181 us -> 178 us (0.983); the launches traced: 178 us -> 178 us
  other arithmetic: 14.4 us -> 11.5 us
  Pallas kernels: 136 us -> 138 us
    select_n x4 -> x3, other arithmetic: 10.6 us -> 3.64 us  [the longest x2 3.64 us: per_device(): outgoing = jnp.take(padded_rhs, line_of_slot, axis=0)]
    transpose x0 -> x1, other arithmetic: none -> 5 us  [per_device(): residual.transpose(1, 2, 0, 3).reshape(line_count, fields * points)]
    pallas_call x1 -> x0, local copies, waits for them, and re-layouts: 3.55 us -> none  [owner_solve(): pl.pallas_call(functools.partial(owner_kernel, peers, group), out_shape=j...]
    add x0 -> x1, local copies, waits for them, and re-layouts: none -> 1.9 us  [per_device(): return adjoint + correction]
    pallas_call x1, Pallas kernels: 136 us -> 138 us  [owner_solve(): pl.pallas_call(functools.partial(owner_kernel, peers, group), out_shape=j...]
    gather x2 -> x3, local copies, waits for them, and re-layouts: 5.84 us -> 7.11 us  [the longest x2 4.06 us: per_device(): correction = jnp.take(returned, slot_ids, axis=0)]
where the time goes in v5:
time: 178 us
  Pallas kernels  138 us (78%)
  local copies, waits for them, and re-layouts  19.2 us (11%)
  other arithmetic  11.5 us (6%)
  starting transfers between devices  7.24 us (4%)
    pallas_call x1, Pallas kernels, owner_solve(): pl.pallas_call(functools.partial(owner_kernel, peers, group), out_shape=j...  138 us
    ppermute x2, starting transfers between devices, extended(): lax.ppermute(lax.slice_in_dim(block, block.shape[dim] - width, None, axis...  5.86 us
    transpose x1, other arithmetic, per_device(): residual.transpose(1, 2, 0, 3).reshape(line_count, fields * points)  5 us
    gather x2, local copies, waits for them, and re-layouts, per_device(): correction = jnp.take(returned, slot_ids, axis=0)  4.06 us
    select_n x2, other arithmetic, per_device(): outgoing = jnp.take(padded_rhs, line_of_slot, axis=0)  3.64 us
  transfers between devices with their start and end apart: 4, of which 1 were waited for; matrix products, arithmetic and copies ran while one was open for 4% of the time, Pallas kernels for 0%

profile of v5, /device:TPU:25, one launch (start us, length us, event | category | flops | bytes accessed | tf_op | source)
XLA Modules:
  0.0 177.6 jit_solution(16760004244711184384)
XLA Ops:
  0.0 0.8 fusion.6
  0.8 1.9 %collective-permute-start.1 = (f32[5,1,4,512]{3,2,1,0:T(4,128)S(1)}, f32[5,1,4,512]{3,2,1,0:T(4,128)S(1)}, u32[]{:S(2)}, u32[]{:S(2)}) collective-permute-start(f32[5,1,4,512]{3,2,1,0:T(4,128)S(1)} %get-tuple-element.45), channel_id=1, source_target_pairs={{0,4},{4,8},{8,12},{12,16},{16,20},{20,24},{24,28},{28,32},{32,36}... | collective-permute-start | bytes 122888 | tf_op jit(solution)/shard_map/ppermute | solution.py:18
  2.7 0.1 collective-permute-start
  2.8 2.5 %fusion.7 = (f32[5,32,1,512]{3,2,1,0:T(1,128)S(1)}, f32[5,32,1,512]{3,2,1,0:T(1,128)S(1)}) fusion(f32[5,32,4,512]{3,2,1,0:T(4,128)} %param.9), kind=kLoop, calls=%fused_computation.70 | loop fusion | bytes 1310720 | tf_op jit(solution)/shard_map/slice | solution.py:21
  5.3 1.3 collective-permute-start.2
  6.6 4.0 %collective-permute-start.3 = (f32[5,32,1,512]{3,1,2,0:T(8,128)S(1)}, f32[5,32,1,512]{3,1,2,0:T(8,128)S(1)}, u32[]{:S(2)}, u32[]{:S(2)}) collective-permute-start(f32[5,32,1,512]{3,1,2,0:T(8,128)S(1)} %copy.66), channel_id=1, source_target_pairs={{0,1},{1,2},{2,3},{4,5},{5,6},{6,7},{8,9},{9,10},{10,11},{12,13},{... | collective-permute-start | bytes 983048 | tf_op jit(solution)/shard_map/ppermute | solution.py:18
  10.6 0.0 copy-done.6
  10.6 0.4 slice_reduce_fusion.19
  11.0 0.2 slice_reduce_fusion.1
  11.2 0.0 copy-done.7
  11.2 0.1 copy.49
  11.3 0.1 copy.51
  11.4 0.1 mul.373
  11.5 0.1 reshape.87
  11.6 0.2 convert_reduce_fusion
  11.8 1.2 scatter_custom_fusion
  13.0 0.1 reduce_sum.14
  13.1 0.0 copy-done.8
  13.1 0.1 copy.52
  13.2 0.1 iota_compare_fusion
  13.3 0.1 copy.50
  13.4 0.0 collective-permute-done.1
  13.4 0.6 constant_dynamic-update-slice_fusion.1
  14.1 0.0 collective-permute-done
  14.1 0.2 slice_bitcast_fusion.9
  14.3 0.2 slice_bitcast_fusion.4
  14.6 1.4 collective-permute-done.2
  16.0 0.3 copy.54
  16.3 0.8 maximum_bitcast_fusion.7
  17.1 0.0 collective-permute-done.3
  17.1 0.3 copy.56
  17.5 0.0 copy-start.4
  17.5 0.0 copy-start.5
  17.5 0.6 maximum_bitcast_fusion.3
  18.1 0.7 copy-done.4
  18.8 0.0 copy-done.5
  18.8 5.0 %select_bitcast_fusion = f32[32,4,5,512]{3,1,0,2:T(4,128)S(1)} fusion(f32[5,32,4,512]{3,2,1,0:T(4,128)S(1)} %copy-done.4, f32[5,32,4,512]{3,2,1,0:T(4,128)S(1)} %copy-done.2, f32[32,4,512]{2,1,0:T(4,128)S(1)} %get-tuple-element.32, f32[5]{0:T(128)S(1)} %get-tuple-element.23, f32[32,4,512]{2,1,0:T(4,128)S(1)} %get-tuple-element.33, ...), kind=kLoop, calls=%fused_computation.6 | loop fusion | flops 14090240 | bytes 9503120 | tf_op jit(solution)/shard_map/transpose | solution.py:301
  23.8 0.8 copy.57
  24.6 1.0 copy.61
  25.7 0.1 concatenate.21
  25.8 3.1 %gather_fusion = f32[256,2560]{1,0:T(8,128)} fusion(f32[129,2560]{1,0:T(8,128)S(1)} %concatenate.21, s32[1024]{0:T(1024)S(1)} %get-tuple-element.51), kind=kCustom, calls=%fused_computation | custom fusion | bytes 5243904 | tf_op jit(solution)/shard_map/jit(_take)/gather | solution.py:312
  28.9 3.6 %broadcast_select_fusion.rhs_ref = f32[256,2560]{1,0:T(8,128)} fusion(f32[256,2560]{1,0:T(8,128)} %gather_fusion, pred[256]{0:T(512)(128)(4,1)S(1)} %compare_and_fusion), kind=kLoop, calls=%fused_computation.5 | loop fusion | flops 655360 | bytes 5243136 | tf_op jit(solution)/shard_map/jit(_take)/select_n | solution.py:312
  32.5 137.9 %shard_map.91 = f32[256,2560]{1,0:T(8,128)S(1)} custom-call(f32[256,2560]{1,0:T(8,128)} %broadcast_select_fusion.rhs_ref, bf16[5,256,512]{2,1,0:T(8,128)(2,1)S(1)} %bitcast.71, bf16[5,256,512]{2,1,0:T(8,128)(2,1)S(1)} %bitcast.72, bf16[25,256,512]{2,1,0:T(8,128)(2,1)} %bitcast.74), custom_call_target="tpu_custom_call" | custom-call | tf_op jit(solution)/shard_map/pallas_call | solution.py:254
  170.4 2.1 %gather_fusion.1 = f32[128,2560]{1,0:T(8,128)} fusion(f32[256,2560]{1,0:T(8,128)S(1)} %shard_map.91, s32[1024]{0:T(1024)S(1)} %get-tuple-element.50), kind=kCustom, calls=%fused_computation.1 | custom fusion | bytes 2621952 | tf_op jit(solution)/shard_map/jit(_take)/gather | solution.py:320
  172.5 2.0 %gather.12 = f32[32,4,5,512]{3,2,1,0:T(8,128)S(1)} reshape(f32[128,2560]{1,0:T(8,128)} %gather_fusion.1) | data formatting | bytes 2621440 | tf_op jit(solution)/shard_map/jit(_take)/gather | solution.py:320
  174.5 0.0 copy-done.3
  174.5 1.2 bitcast_add_fusion
  175.7 1.9 %copy.60 = f32[5,32,4,512]{3,2,1,0:T(4,128)} copy(f32[5,32,4,512]{3,1,2,0:T(8,128)S(1)} %bitcast_add_fusion) | data formatting | bytes 2621440 | tf_op jit(solution)/shard_map/add | solution.py:322
  (21 shorter events, 0.1 us)
Async XLA Ops:
  0.8 12.6 %collective-permute-start.1 = (f32[5,1,4,512]{3,2,1,0:T(4,128)S(1)}, f32[5,1,4,512]{3,2,1,0:T(4,128)S(1)}, u32[]{:S(2)}, u32[]{:S(2)}) collective-permute-start(f32[5,1,4,512]{3,2,1,0:T(4,128)S(1)} %get-tuple-element.45), channel_id=1, source_target_pairs={{0,4},{4,8},{8,12},{12,16},{16,20},{20,24},{24,28},{28,32},{32,36}... | collective-permute-start | bytes 122888 | tf_op jit(solution)/shard_map/ppermute | solution.py:18
  2.7 8.0 %copy-start.6 = (f32[4,5,5]{2,0,1:T(4,128)S(1)}, f32[4,5,5]{2,0,1:T(4,128)}, u32[]{:S(2)}) copy-start(f32[4,5,5]{2,0,1:T(4,128)} %param.14) | copy-start | bytes 1204
  2.7 8.5 %copy-start.7 = (s32[1,32,4,1]{1,3,2,0:T(1,128)S(1)}, s32[1,32,4,1]{1,3,2,0:T(1,128)}, u32[]{:S(2)}) copy-start(s32[1,32,4,1]{1,3,2,0:T(1,128)} %param.13) | copy-start | bytes 1540
  2.7 10.4 %copy-start.8 = (s32[32,4]{0,1:T(4,128)S(1)}, s32[32,4]{0,1:T(4,128)}, u32[]{:S(2)}) copy-start(s32[32,4]{0,1:T(4,128)} %param.12) | copy-start | bytes 1540
  2.7 10.8 %copy-start.2 = (f32[5,32,4,512]{3,2,1,0:T(4,128)S(1)}, f32[5,32,4,512]{3,2,1,0:T(4,128)}, u32[]{:S(2)}) copy-start(f32[5,32,4,512]{3,2,1,0:T(4,128)} %param.9) | copy-start | bytes 3932164
  2.7 11.4 %collective-permute-start = (f32[5,1,4,512]{3,2,1,0:T(4,128)S(1)}, f32[5,1,4,512]{3,2,1,0:T(4,128)S(1)}, u32[]{:S(2)}, u32[]{:S(2)}) collective-permute-start(f32[5,1,4,512]{3,2,1,0:T(4,128)S(1)} %get-tuple-element.44), channel_id=1, source_target_pairs={{4,0},{8,4},{12,8},{16,12},{20,16},{24,20},{28,24},{32,28},{36,32}... | collective-permute-start | bytes 122888 | tf_op jit(solution)/shard_map/ppermute | solution.py:21
  5.3 10.7 %collective-permute-start.2 = (f32[5,32,1,512]{3,1,2,0:T(8,128)S(1)}, f32[5,32,1,512]{3,1,2,0:T(8,128)S(1)}, u32[]{:S(2)}, u32[]{:S(2)}) collective-permute-start(f32[5,32,1,512]{3,1,2,0:T(8,128)S(1)} %copy.67), channel_id=1, source_target_pairs={{1,0},{2,1},{3,2},{5,4},{6,5},{7,6},{9,8},{10,9},{11,10},{13,12},{... | collective-permute-start | bytes 983048 | tf_op jit(solution)/shard_map/ppermute | solution.py:21
  6.6 10.5 %collective-permute-start.3 = (f32[5,32,1,512]{3,1,2,0:T(8,128)S(1)}, f32[5,32,1,512]{3,1,2,0:T(8,128)S(1)}, u32[]{:S(2)}, u32[]{:S(2)}) collective-permute-start(f32[5,32,1,512]{3,1,2,0:T(8,128)S(1)} %copy.66), channel_id=1, source_target_pairs={{0,1},{1,2},{2,3},{4,5},{5,6},{6,7},{8,9},{9,10},{10,11},{12,13},{... | collective-permute-start | bytes 983048 | tf_op jit(solution)/shard_map/ppermute | solution.py:18
  17.5 1.3 copy-start.4
  17.5 1.3 copy-start.5
  28.9 3.6 %copy-start = (bf16[1,256,5,512]{3,1,2,0:T(8,128)(2,1)S(1)}, bf16[1,256,5,512]{3,1,2,0:T(8,128)(2,1)}, u32[]{:S(2)}) copy-start(bf16[1,256,5,512]{3,1,2,0:T(8,128)(2,1)} %param.15) | copy-start | bytes 3932164
  28.9 3.6 %copy-start.1 = (bf16[1,256,5,512]{3,1,2,0:T(8,128)(2,1)S(1)}, bf16[1,256,5,512]{3,1,2,0:T(8,128)(2,1)}, u32[]{:S(2)}) copy-start(bf16[1,256,5,512]{3,1,2,0:T(8,128)(2,1)} %param.16) | copy-start | bytes 3932164
  172.5 2.0 %copy-start.3 = (f32[5,32,4,512]{3,2,1,0:T(4,128)S(1)}, f32[5,32,4,512]{3,2,1,0:T(4,128)}, u32[]{:S(2)}) copy-start(f32[5,32,4,512]{3,2,1,0:T(4,128)} %param.9) | copy-start | bytes 3932164

commit v6 on v5

--- a/solution.py
+++ b/solution.py
@@ -46,74 +46,6 @@
 
 
 MESH = pl.DeviceIdType.MESH
-
-
-def exchange_kernel(peers, x_ref, o_ref, send_sems, recv_sems, local_sem):
-    width = x_ref.shape[1] // peers
-    me = lax.axis_index("circ")
-    plane = lax.axis_index("ax")
-    barrier = pltpu.get_barrier_semaphore()
-
-    def greet(i, carry):
-        peer = lax.rem(me + i, peers)
-        pl.semaphore_signal(barrier, inc=1, device_id=(peer, plane), device_id_type=MESH)
-        return carry
-
-    lax.fori_loop(1, peers, greet, 0)
-    pl.semaphore_wait(barrier, peers - 1)
-    own = pl.ds(me * width, width)
-    local = pltpu.make_async_copy(x_ref.at[:, own], o_ref.at[:, own], local_sem)
-    local.start()
-
-    def outgoing(i):
-        peer = lax.rem(me + i, peers)
-        return pltpu.make_async_remote_copy(
-            src_ref=x_ref.at[:, pl.ds(peer * width, width)],
-            dst_ref=o_ref.at[:, pl.ds(me * width, width)],
-            send_sem=send_sems.at[peer],
-            recv_sem=recv_sems.at[me],
-            device_id=(peer, plane),
-            device_id_type=MESH,
-        )
-
-    def incoming(i):
-        peer = lax.rem(me + peers - i, peers)
-        return pltpu.make_async_remote_copy(
-            src_ref=x_ref.at[:, pl.ds(me * width, width)],
-            dst_ref=o_ref.at[:, pl.ds(peer * width, width)],
-            send_sem=send_sems.at[me],
-            recv_sem=recv_sems.at[peer],
-            device_id=(peer, plane),
-            device_id_type=MESH,
-        )
-
-    def start(i, carry):
-        outgoing(i).start()
-        return carry
-
-    def finish(i, carry):
-        outgoing(i).wait_send()
-        incoming(i).wait_recv()
-        return carry
-
-    lax.fori_loop(1, peers, start, 0)
-    local.wait()
-    lax.fori_loop(1, peers, finish, 0)
-
-
-def exchange(chunks, peers, collective_id):
-    return pl.pallas_call(
-        functools.partial(exchange_kernel, peers),
-        out_shape=jax.ShapeDtypeStruct(chunks.shape, chunks.dtype),
-        in_specs=[pl.BlockSpec(memory_space=pl.ANY)],
-        out_specs=pl.BlockSpec(memory_space=pl.ANY),
-        scratch_shapes=[
-            pltpu.SemaphoreType.DMA((peers,)),
-            pltpu.SemaphoreType.DMA((peers,)),
-            pltpu.SemaphoreType.DMA(()),
-        ],
-        compiler_params=pltpu.CompilerParams(collective_id=collective_id, has_side_effects=True),
-    )(chunks)
 
 
 def solve_rows(rhs, lower, upper, pivot):
@@ -134,7 +66,7 @@
 
 
 def owner_kernel(
-    peers, group, rhs_ref, lower_ref, upper_ref, pivot_ref, out_ref,
+    peers, group, ahead, rhs_ref, lower_ref, upper_ref, pivot_ref, out_ref,
     rhs_in, solved, lower_v, upper_v, pivot_v,
     send_rhs, recv_rhs, send_sol, recv_sol, local_sems,
 ):
@@ -188,24 +120,40 @@
     own_rhs = pltpu.make_async_copy(rhs_ref.at[window(me)], rhs_in.at[window(me)], local_sems.at[3])
     own_sol = pltpu.make_async_copy(solved.at[window(me)], out_ref.at[window(me)], local_sems.at[4])
 
-    def send(i, carry):
-        target = group * lax.rem(mine - i // group + groups, groups) + i % group
-
-        @pl.when(target == me)
-        def _():
-            own_rhs.start()
-
-        @pl.when(target != me)
-        def _():
-            rhs_copy(me, target).start()
-
-        return carry
-
-    lax.fori_loop(0, peers, send, 0)
+    def target_of(step, r):
+        return group * lax.rem(mine - step + groups, groups) + r
+
+    def send_step(step):
+        for r in range(group):
+            target = target_of(step, r)
+
+            @pl.when(target == me)
+            def _():
+                own_rhs.start()
+
+            @pl.when(target != me)
+            def _():
+                rhs_copy(me, target).start()
+
+    def sent_step(step):
+        for r in range(group):
+            target = target_of(step, r)
+
+            @pl.when(target != me)
+            def _():
+                rhs_copy(me, target).wait_send()
+
+    for step in range(min(ahead, groups)):
+        send_step(step)
     for copy in factor_copies:
         copy.wait()
 
     def solve(j, carry):
+        @pl.when(j + ahead < groups)
+        def _():
+            sent_step(j)
+            send_step(j + ahead)
+
         g = lax.rem(mine + j, groups)
         for r in range(group):
             source = g * group + r
@@ -238,10 +186,11 @@
         return carry
 
     lax.fori_loop(0, groups, solve, 0)
+    for step in range(max(groups - ahead, 0), groups):
+        sent_step(step)
 
     def finish(i, carry):
         peer = lax.rem(me + i, peers)
-        rhs_copy(me, peer).wait_send()
         sol_copy(me, peer).wait_send()
         sol_copy(peer, me).wait_recv()
         return carry
@@ -250,9 +199,9 @@
     own_sol.wait()
 
 
-def owner_solve(rhs, lower, upper, pivot, peers, group=4):
+def owner_solve(rhs, lower, upper, pivot, peers, group=4, ahead=3):
     return pl.pallas_call(
-        functools.partial(owner_kernel, peers, group),
+        functools.partial(owner_kernel, peers, group, ahead),
         out_shape=jax.ShapeDtypeStruct(rhs.shape, rhs.dtype),
         in_specs=[pl.BlockSpec(memory_space=pl.ANY)] * 4,
         out_specs=pl.BlockSpec(memory_space=pl.ANY),

time: 178 us -> 201 us (1.13)
  Pallas kernels: 138 us -> 159 us
    pallas_call x1, Pallas kernels: 138 us -> 159 us  [owner_solve(): pl.pallas_call(functools.partial(owner_kernel, peers, group, ahead), out_...]
where the time goes in v6:
time: 201 us; the launch traced here: 199 us
  Pallas kernels  159 us (79%)
  local copies, waits for them, and re-layouts  19.2 us (10%)
  other arithmetic  11.5 us (6%)
  starting transfers between devices  7.24 us (4%)
    pallas_call x1, Pallas kernels, owner_solve(): pl.pallas_call(functools.partial(owner_kernel, peers, group, ahead), out_...  159 us
    ppermute x2, starting transfers between devices, extended(): lax.ppermute(lax.slice_in_dim(block, block.shape[dim] - width, None, axis...  5.86 us
    transpose x1, other arithmetic, per_device(): residual.transpose(1, 2, 0, 3).reshape(line_count, fields * points)  5 us
    gather x2, local copies, waits for them, and re-layouts, per_device(): correction = jnp.take(returned, slot_ids, axis=0)  4.06 us
  transfers between devices with their start and end apart: 4, of which 1 were waited for; matrix products, arithmetic and copies ran while one was open for 4% of the time, Pallas kernels for 0%

profile of v6, /device:TPU:25, one launch (start us, length us, event | category | flops | bytes accessed | tf_op | source)
XLA Modules:
  0.0 199.0 jit_solution(18382862566157448504)
XLA Ops:
  0.0 0.8 fusion.6
  0.8 1.9 collective-permute-start.1
  2.7 0.1 collective-permute-start
  2.8 2.5 %fusion.7 = (f32[5,32,1,512]{3,2,1,0:T(1,128)S(1)}, f32[5,32,1,512]{3,2,1,0:T(1,128)S(1)}) fusion(f32[5,32,4,512]{3,2,1,0:T(4,128)} %param.9), kind=kLoop, calls=%fused_computation.70 | loop fusion | bytes 1310720 | tf_op jit(solution)/shard_map/slice | solution.py:21
  5.3 1.3 collective-permute-start.2
  6.6 4.0 %collective-permute-start.3 = (f32[5,32,1,512]{3,1,2,0:T(8,128)S(1)}, f32[5,32,1,512]{3,1,2,0:T(8,128)S(1)}, u32[]{:S(2)}, u32[]{:S(2)}) collective-permute-start(f32[5,32,1,512]{3,1,2,0:T(8,128)S(1)} %copy.66), channel_id=1, source_target_pairs={{0,1},{1,2},{2,3},{4,5},{5,6},{6,7},{8,9},{9,10},{10,11},{12,13},{... | collective-permute-start | bytes 983048 | tf_op jit(solution)/shard_map/ppermute | solution.py:18
  10.6 0.0 copy-done.6
  10.6 0.4 slice_reduce_fusion.19
  11.0 0.2 slice_reduce_fusion.1
  11.2 0.0 copy-done.7
  11.2 0.1 copy.49
  11.3 0.1 copy.51
  11.4 0.1 mul.373
  11.5 0.1 reshape.87
  11.6 0.2 convert_reduce_fusion
  11.8 1.2 scatter_custom_fusion
  13.0 0.1 reduce_sum.14
  13.1 0.0 copy-done.8
  13.1 0.1 copy.52
  13.2 0.1 iota_compare_fusion
  13.3 0.1 copy.50
  13.4 0.0 collective-permute-done.1
  13.4 0.0 copy-done.2
  13.4 0.6 constant_dynamic-update-slice_fusion.1
  14.1 0.0 collective-permute-done
  14.1 0.2 slice_bitcast_fusion.9
  14.3 0.2 slice_bitcast_fusion.4
  14.6 1.4 collective-permute-done.2
  16.0 0.3 copy.54
  16.3 0.8 maximum_bitcast_fusion.7
  17.1 0.0 collective-permute-done.3
  17.1 0.3 copy.56
  17.5 0.0 copy-start.4
  17.5 0.0 copy-start.5
  17.5 0.6 maximum_bitcast_fusion.3
  18.1 0.7 copy-done.4
  18.8 0.0 copy-done.5
  18.8 5.0 %select_bitcast_fusion = f32[32,4,5,512]{3,1,0,2:T(4,128)S(1)} fusion(f32[5,32,4,512]{3,2,1,0:T(4,128)S(1)} %copy-done.4, f32[5,32,4,512]{3,2,1,0:T(4,128)S(1)} %copy-done.2, f32[32,4,512]{2,1,0:T(4,128)S(1)} %get-tuple-element.32, f32[5]{0:T(128)S(1)} %get-tuple-element.23, f32[32,4,512]{2,1,0:T(4,128)S(1)} %get-tuple-element.33, ...), kind=kLoop, calls=%fused_computation.6 | loop fusion | flops 14090240 | bytes 9503120 | tf_op jit(solution)/shard_map/transpose | solution.py:250
  23.8 0.8 copy.57
  24.6 1.0 copy.61
  25.7 0.1 concatenate.21
  25.8 3.1 %gather_fusion = f32[256,2560]{1,0:T(8,128)} fusion(f32[129,2560]{1,0:T(8,128)S(1)} %concatenate.21, s32[1024]{0:T(1024)S(1)} %get-tuple-element.51), kind=kCustom, calls=%fused_computation | custom fusion | bytes 5243904 | tf_op jit(solution)/shard_map/jit(_take)/gather | solution.py:261
  28.9 3.6 %broadcast_select_fusion.rhs_ref = f32[256,2560]{1,0:T(8,128)} fusion(f32[256,2560]{1,0:T(8,128)} %gather_fusion, pred[256]{0:T(512)(128)(4,1)S(1)} %compare_and_fusion), kind=kLoop, calls=%fused_computation.5 | loop fusion | flops 655360 | bytes 5243136 | tf_op jit(solution)/shard_map/jit(_take)/select_n | solution.py:261
  32.5 159.3 %shard_map.91 = f32[256,2560]{1,0:T(8,128)S(1)} custom-call(f32[256,2560]{1,0:T(8,128)} %broadcast_select_fusion.rhs_ref, bf16[5,256,512]{2,1,0:T(8,128)(2,1)S(1)} %bitcast.71, bf16[5,256,512]{2,1,0:T(8,128)(2,1)S(1)} %bitcast.72, bf16[25,256,512]{2,1,0:T(8,128)(2,1)} %bitcast.74), custom_call_target="tpu_custom_call" | custom-call | tf_op jit(solution)/shard_map/pallas_call | solution.py:203
  191.8 2.1 %gather_fusion.1 = f32[128,2560]{1,0:T(8,128)} fusion(f32[256,2560]{1,0:T(8,128)S(1)} %shard_map.91, s32[1024]{0:T(1024)S(1)} %get-tuple-element.50), kind=kCustom, calls=%fused_computation.1 | custom fusion | bytes 2621952 | tf_op jit(solution)/shard_map/jit(_take)/gather | solution.py:269
  193.9 2.0 gather.12
  195.9 1.2 bitcast_add_fusion
  197.1 1.9 copy.60
  (21 shorter events, 0.1 us)
Async XLA Ops:
  0.8 12.6 %collective-permute-start.1 = (f32[5,1,4,512]{3,2,1,0:T(4,128)S(1)}, f32[5,1,4,512]{3,2,1,0:T(4,128)S(1)}, u32[]{:S(2)}, u32[]{:S(2)}) collective-permute-start(f32[5,1,4,512]{3,2,1,0:T(4,128)S(1)} %get-tuple-element.45), channel_id=1, source_target_pairs={{0,4},{4,8},{8,12},{12,16},{16,20},{20,24},{24,28},{28,32},{32,36}... | collective-permute-start | bytes 122888 | tf_op jit(solution)/shard_map/ppermute | solution.py:18
  2.7 8.0 %copy-start.6 = (f32[4,5,5]{2,0,1:T(4,128)S(1)}, f32[4,5,5]{2,0,1:T(4,128)}, u32[]{:S(2)}) copy-start(f32[4,5,5]{2,0,1:T(4,128)} %param.14) | copy-start | bytes 1204
  2.7 8.5 %copy-start.7 = (s32[1,32,4,1]{1,3,2,0:T(1,128)S(1)}, s32[1,32,4,1]{1,3,2,0:T(1,128)}, u32[]{:S(2)}) copy-start(s32[1,32,4,1]{1,3,2,0:T(1,128)} %param.13) | copy-start | bytes 1540
  2.7 10.4 %copy-start.8 = (s32[32,4]{0,1:T(4,128)S(1)}, s32[32,4]{0,1:T(4,128)}, u32[]{:S(2)}) copy-start(s32[32,4]{0,1:T(4,128)} %param.12) | copy-start | bytes 1540
  2.7 10.8 %copy-start.2 = (f32[5,32,4,512]{3,2,1,0:T(4,128)S(1)}, f32[5,32,4,512]{3,2,1,0:T(4,128)}, u32[]{:S(2)}) copy-start(f32[5,32,4,512]{3,2,1,0:T(4,128)} %param.9) | copy-start | bytes 3932164
  2.7 11.4 %collective-permute-start = (f32[5,1,4,512]{3,2,1,0:T(4,128)S(1)}, f32[5,1,4,512]{3,2,1,0:T(4,128)S(1)}, u32[]{:S(2)}, u32[]{:S(2)}) collective-permute-start(f32[5,1,4,512]{3,2,1,0:T(4,128)S(1)} %get-tuple-element.44), channel_id=1, source_target_pairs={{4,0},{8,4},{12,8},{16,12},{20,16},{24,20},{28,24},{32,28},{36,32}... | collective-permute-start | bytes 122888 | tf_op jit(solution)/shard_map/ppermute | solution.py:21
  5.3 10.7 %collective-permute-start.2 = (f32[5,32,1,512]{3,1,2,0:T(8,128)S(1)}, f32[5,32,1,512]{3,1,2,0:T(8,128)S(1)}, u32[]{:S(2)}, u32[]{:S(2)}) collective-permute-start(f32[5,32,1,512]{3,1,2,0:T(8,128)S(1)} %copy.67), channel_id=1, source_target_pairs={{1,0},{2,1},{3,2},{5,4},{6,5},{7,6},{9,8},{10,9},{11,10},{13,12},{... | collective-permute-start | bytes 983048 | tf_op jit(solution)/shard_map/ppermute | solution.py:21
  6.6 10.5 %collective-permute-start.3 = (f32[5,32,1,512]{3,1,2,0:T(8,128)S(1)}, f32[5,32,1,512]{3,1,2,0:T(8,128)S(1)}, u32[]{:S(2)}, u32[]{:S(2)}) collective-permute-start(f32[5,32,1,512]{3,1,2,0:T(8,128)S(1)} %copy.66), channel_id=1, source_target_pairs={{0,1},{1,2},{2,3},{4,5},{5,6},{6,7},{8,9},{9,10},{10,11},{12,13},{... | collective-permute-start | bytes 983048 | tf_op jit(solution)/shard_map/ppermute | solution.py:18
  17.5 1.3 copy-start.4
  17.5 1.3 copy-start.5
  28.9 3.6 %copy-start = (bf16[1,256,5,512]{3,1,2,0:T(8,128)(2,1)S(1)}, bf16[1,256,5,512]{3,1,2,0:T(8,128)(2,1)}, u32[]{:S(2)}) copy-start(bf16[1,256,5,512]{3,1,2,0:T(8,128)(2,1)} %param.15) | copy-start | bytes 3932164
  28.9 3.6 %copy-start.1 = (bf16[1,256,5,512]{3,1,2,0:T(8,128)(2,1)S(1)}, bf16[1,256,5,512]{3,1,2,0:T(8,128)(2,1)}, u32[]{:S(2)}) copy-start(bf16[1,256,5,512]{3,1,2,0:T(8,128)(2,1)} %param.16) | copy-start | bytes 3932164
  193.9 2.0 copy-start.3

commit v7 on v6

--- a/solution.py
+++ b/solution.py
@@ -66,7 +66,7 @@
 
 
 def owner_kernel(
-    peers, group, ahead, rhs_ref, lower_ref, upper_ref, pivot_ref, out_ref,
+    peers, group, rhs_ref, lower_ref, upper_ref, pivot_ref, out_ref,
     rhs_in, solved, lower_v, upper_v, pivot_v,
     send_rhs, recv_rhs, send_sol, recv_sol, local_sems,
 ):
@@ -120,41 +120,29 @@
     own_rhs = pltpu.make_async_copy(rhs_ref.at[window(me)], rhs_in.at[window(me)], local_sems.at[3])
     own_sol = pltpu.make_async_copy(solved.at[window(me)], out_ref.at[window(me)], local_sems.at[4])
 
-    def target_of(step, r):
-        return group * lax.rem(mine - step + groups, groups) + r
-
-    def send_step(step):
-        for r in range(group):
-            target = target_of(step, r)
-
-            @pl.when(target == me)
-            def _():
-                own_rhs.start()
-
-            @pl.when(target != me)
-            def _():
-                rhs_copy(me, target).start()
-
-    def sent_step(step):
-        for r in range(group):
-            target = target_of(step, r)
-
-            @pl.when(target != me)
-            def _():
-                rhs_copy(me, target).wait_send()
-
-    for step in range(min(ahead, groups)):
-        send_step(step)
+    def order(step):
+        half = step // 2
+        return lax.select(step % 2 == 0, half, groups - 1 - half)
+
+    def send(i, carry):
+        target = group * lax.rem(mine - order(i // group) + groups, groups) + i % group
+
+        @pl.when(target == me)
+        def _():
+            own_rhs.start()
+
+        @pl.when(target != me)
+        def _():
+            rhs_copy(me, target).start()
+
+        return carry
+
+    lax.fori_loop(0, peers, send, 0)
     for copy in factor_copies:
         copy.wait()
 
     def solve(j, carry):
-        @pl.when(j + ahead < groups)
-        def _():
-            sent_step(j)
-            send_step(j + ahead)
-
-        g = lax.rem(mine + j, groups)
+        g = lax.rem(mine + order(j), groups)
         for r in range(group):
             source = g * group + r
 
@@ -186,11 +174,10 @@
         return carry
 
     lax.fori_loop(0, groups, solve, 0)
-    for step in range(max(groups - ahead, 0), groups):
-        sent_step(step)
 
     def finish(i, carry):
         peer = lax.rem(me + i, peers)
+        rhs_copy(me, peer).wait_send()
         sol_copy(me, peer).wait_send()
         sol_copy(peer, me).wait_recv()
         return carry
@@ -199,9 +186,9 @@
     own_sol.wait()
 
 
-def owner_solve(rhs, lower, upper, pivot, peers, group=4, ahead=3):
+def owner_solve(rhs, lower, upper, pivot, peers, group=4):
     return pl.pallas_call(
-        functools.partial(owner_kernel, peers, group, ahead),
+        functools.partial(owner_kernel, peers, group),
         out_shape=jax.ShapeDtypeStruct(rhs.shape, rhs.dtype),
         in_specs=[pl.BlockSpec(memory_space=pl.ANY)] * 4,
         out_specs=pl.BlockSpec(memory_space=pl.ANY),

time: 201 us -> 171 us (0.85)
  Pallas kernels: 159 us -> 130 us
    pallas_call x1, Pallas kernels: 159 us -> 130 us  [owner_solve(): pl.pallas_call(functools.partial(owner_kernel, peers, group), out_shape=j...]
where the time goes in v7:
time: 171 us; the launch traced here: 170 us
  Pallas kernels  130 us (76%)
  local copies, waits for them, and re-layouts  19.2 us (11%)
  other arithmetic  11.5 us (7%)
  starting transfers between devices  7.24 us (4%)
    pallas_call x1, Pallas kernels, owner_solve(): pl.pallas_call(functools.partial(owner_kernel, peers, group), out_shape=j...  130 us
    ppermute x2, starting transfers between devices, extended(): lax.ppermute(lax.slice_in_dim(block, block.shape[dim] - width, None, axis...  5.86 us
    transpose x1, other arithmetic, per_device(): residual.transpose(1, 2, 0, 3).reshape(line_count, fields * points)  5 us
    gather x2, local copies, waits for them, and re-layouts, per_device(): correction = jnp.take(returned, slot_ids, axis=0)  4.06 us
    select_n x2, other arithmetic, per_device(): outgoing = jnp.take(padded_rhs, line_of_slot, axis=0)  3.64 us
  transfers between devices with their start and end apart: 4, of which 1 were waited for; matrix products, arithmetic and copies ran while one was open for 4% of the time, Pallas kernels for 0%

profile of v7, /device:TPU:25, one launch (start us, length us, event | category | flops | bytes accessed | tf_op | source)
XLA Modules:
  0.0 169.7 jit_solution(11955806889877606364)
XLA Ops:
  0.0 0.8 fusion.6
  0.8 1.9 %collective-permute-start.1 = (f32[5,1,4,512]{3,2,1,0:T(4,128)S(1)}, f32[5,1,4,512]{3,2,1,0:T(4,128)S(1)}, u32[]{:S(2)}, u32[]{:S(2)}) collective-permute-start(f32[5,1,4,512]{3,2,1,0:T(4,128)S(1)} %get-tuple-element.45), channel_id=1, source_target_pairs={{0,4},{4,8},{8,12},{12,16},{16,20},{20,24},{24,28},{28,32},{32,36}... | collective-permute-start | bytes 122888 | tf_op jit(solution)/shard_map/ppermute | solution.py:18
  2.7 0.1 collective-permute-start
  2.8 2.5 %fusion.7 = (f32[5,32,1,512]{3,2,1,0:T(1,128)S(1)}, f32[5,32,1,512]{3,2,1,0:T(1,128)S(1)}) fusion(f32[5,32,4,512]{3,2,1,0:T(4,128)} %param.9), kind=kLoop, calls=%fused_computation.70 | loop fusion | bytes 1310720 | tf_op jit(solution)/shard_map/slice | solution.py:21
  5.3 1.3 collective-permute-start.2
  6.6 4.0 %collective-permute-start.3 = (f32[5,32,1,512]{3,1,2,0:T(8,128)S(1)}, f32[5,32,1,512]{3,1,2,0:T(8,128)S(1)}, u32[]{:S(2)}, u32[]{:S(2)}) collective-permute-start(f32[5,32,1,512]{3,1,2,0:T(8,128)S(1)} %copy.66), channel_id=1, source_target_pairs={{0,1},{1,2},{2,3},{4,5},{5,6},{6,7},{8,9},{9,10},{10,11},{12,13},{... | collective-permute-start | bytes 983048 | tf_op jit(solution)/shard_map/ppermute | solution.py:18
  10.6 0.0 copy-done.6
  10.6 0.4 slice_reduce_fusion.19
  11.0 0.2 slice_reduce_fusion.1
  11.2 0.0 copy-done.7
  11.2 0.1 copy.49
  11.3 0.1 copy.51
  11.4 0.1 mul.373
  11.5 0.1 reshape.87
  11.6 0.2 convert_reduce_fusion
  11.8 1.2 scatter_custom_fusion
  13.0 0.1 reduce_sum.14
  13.1 0.0 copy-done.8
  13.1 0.1 copy.52
  13.2 0.1 iota_compare_fusion
  13.3 0.1 copy.50
  13.4 0.0 collective-permute-done.1
  13.4 0.0 copy-done.2
  13.4 0.6 constant_dynamic-update-slice_fusion.1
  14.1 0.0 collective-permute-done
  14.1 0.2 slice_bitcast_fusion.9
  14.3 0.2 slice_bitcast_fusion.4
  14.6 1.4 collective-permute-done.2
  16.0 0.3 copy.54
  16.3 0.8 maximum_bitcast_fusion.7
  17.1 0.0 collective-permute-done.3
  17.1 0.3 copy.56
  17.5 0.0 copy-start.4
  17.5 0.0 copy-start.5
  17.5 0.6 maximum_bitcast_fusion.3
  18.1 0.7 copy-done.4
  18.8 0.0 copy-done.5
  18.8 5.0 %select_bitcast_fusion = f32[32,4,5,512]{3,1,0,2:T(4,128)S(1)} fusion(f32[5,32,4,512]{3,2,1,0:T(4,128)S(1)} %copy-done.4, f32[5,32,4,512]{3,2,1,0:T(4,128)S(1)} %copy-done.2, f32[32,4,512]{2,1,0:T(4,128)S(1)} %get-tuple-element.32, f32[5]{0:T(128)S(1)} %get-tuple-element.23, f32[32,4,512]{2,1,0:T(4,128)S(1)} %get-tuple-element.33, ...), kind=kLoop, calls=%fused_computation.6 | loop fusion | flops 14090240 | bytes 9503120 | tf_op jit(solution)/shard_map/transpose | solution.py:237
  23.8 0.8 copy.57
  24.6 1.0 copy.61
  25.7 0.1 concatenate.21
  25.8 3.1 %gather_fusion = f32[256,2560]{1,0:T(8,128)} fusion(f32[129,2560]{1,0:T(8,128)S(1)} %concatenate.21, s32[1024]{0:T(1024)S(1)} %get-tuple-element.51), kind=kCustom, calls=%fused_computation | custom fusion | bytes 5243904 | tf_op jit(solution)/shard_map/jit(_take)/gather | solution.py:248
  28.9 3.6 %broadcast_select_fusion.rhs_ref = f32[256,2560]{1,0:T(8,128)} fusion(f32[256,2560]{1,0:T(8,128)} %gather_fusion, pred[256]{0:T(512)(128)(4,1)S(1)} %compare_and_fusion), kind=kLoop, calls=%fused_computation.5 | loop fusion | flops 655360 | bytes 5243136 | tf_op jit(solution)/shard_map/jit(_take)/select_n | solution.py:248
  32.5 130.0 %shard_map.91 = f32[256,2560]{1,0:T(8,128)S(1)} custom-call(f32[256,2560]{1,0:T(8,128)} %broadcast_select_fusion.rhs_ref, bf16[5,256,512]{2,1,0:T(8,128)(2,1)S(1)} %bitcast.71, bf16[5,256,512]{2,1,0:T(8,128)(2,1)S(1)} %bitcast.72, bf16[25,256,512]{2,1,0:T(8,128)(2,1)} %bitcast.74), custom_call_target="tpu_custom_call" | custom-call | tf_op jit(solution)/shard_map/pallas_call | solution.py:190
  162.5 2.1 %gather_fusion.1 = f32[128,2560]{1,0:T(8,128)} fusion(f32[256,2560]{1,0:T(8,128)S(1)} %shard_map.91, s32[1024]{0:T(1024)S(1)} %get-tuple-element.50), kind=kCustom, calls=%fused_computation.1 | custom fusion | bytes 2621952 | tf_op jit(solution)/shard_map/jit(_take)/gather | solution.py:256
  164.6 2.0 %gather.12 = f32[32,4,5,512]{3,2,1,0:T(8,128)S(1)} reshape(f32[128,2560]{1,0:T(8,128)} %gather_fusion.1) | data formatting | bytes 2621440 | tf_op jit(solution)/shard_map/jit(_take)/gather | solution.py:256
  166.6 1.2 bitcast_add_fusion
  167.8 1.9 %copy.60 = f32[5,32,4,512]{3,2,1,0:T(4,128)} copy(f32[5,32,4,512]{3,1,2,0:T(8,128)S(1)} %bitcast_add_fusion) | data formatting | bytes 2621440 | tf_op jit(solution)/shard_map/add | solution.py:258
  (21 shorter events, 0.1 us)
Async XLA Ops:
  0.8 12.6 %collective-permute-start.1 = (f32[5,1,4,512]{3,2,1,0:T(4,128)S(1)}, f32[5,1,4,512]{3,2,1,0:T(4,128)S(1)}, u32[]{:S(2)}, u32[]{:S(2)}) collective-permute-start(f32[5,1,4,512]{3,2,1,0:T(4,128)S(1)} %get-tuple-element.45), channel_id=1, source_target_pairs={{0,4},{4,8},{8,12},{12,16},{16,20},{20,24},{24,28},{28,32},{32,36}... | collective-permute-start | bytes 122888 | tf_op jit(solution)/shard_map/ppermute | solution.py:18
  2.7 8.0 %copy-start.6 = (f32[4,5,5]{2,0,1:T(4,128)S(1)}, f32[4,5,5]{2,0,1:T(4,128)}, u32[]{:S(2)}) copy-start(f32[4,5,5]{2,0,1:T(4,128)} %param.14) | copy-start | bytes 1204
  2.7 8.5 %copy-start.7 = (s32[1,32,4,1]{1,3,2,0:T(1,128)S(1)}, s32[1,32,4,1]{1,3,2,0:T(1,128)}, u32[]{:S(2)}) copy-start(s32[1,32,4,1]{1,3,2,0:T(1,128)} %param.13) | copy-start | bytes 1540
  2.7 10.4 %copy-start.8 = (s32[32,4]{0,1:T(4,128)S(1)}, s32[32,4]{0,1:T(4,128)}, u32[]{:S(2)}) copy-start(s32[32,4]{0,1:T(4,128)} %param.12) | copy-start | bytes 1540
  2.7 10.8 %copy-start.2 = (f32[5,32,4,512]{3,2,1,0:T(4,128)S(1)}, f32[5,32,4,512]{3,2,1,0:T(4,128)}, u32[]{:S(2)}) copy-start(f32[5,32,4,512]{3,2,1,0:T(4,128)} %param.9) | copy-start | bytes 3932164
  2.7 11.4 %collective-permute-start = (f32[5,1,4,512]{3,2,1,0:T(4,128)S(1)}, f32[5,1,4,512]{3,2,1,0:T(4,128)S(1)}, u32[]{:S(2)}, u32[]{:S(2)}) collective-permute-start(f32[5,1,4,512]{3,2,1,0:T(4,128)S(1)} %get-tuple-element.44), channel_id=1, source_target_pairs={{4,0},{8,4},{12,8},{16,12},{20,16},{24,20},{28,24},{32,28},{36,32}... | collective-permute-start | bytes 122888 | tf_op jit(solution)/shard_map/ppermute | solution.py:21
  5.3 10.7 %collective-permute-start.2 = (f32[5,32,1,512]{3,1,2,0:T(8,128)S(1)}, f32[5,32,1,512]{3,1,2,0:T(8,128)S(1)}, u32[]{:S(2)}, u32[]{:S(2)}) collective-permute-start(f32[5,32,1,512]{3,1,2,0:T(8,128)S(1)} %copy.67), channel_id=1, source_target_pairs={{1,0},{2,1},{3,2},{5,4},{6,5},{7,6},{9,8},{10,9},{11,10},{13,12},{... | collective-permute-start | bytes 983048 | tf_op jit(solution)/shard_map/ppermute | solution.py:21
  6.6 10.5 %collective-permute-start.3 = (f32[5,32,1,512]{3,1,2,0:T(8,128)S(1)}, f32[5,32,1,512]{3,1,2,0:T(8,128)S(1)}, u32[]{:S(2)}, u32[]{:S(2)}) collective-permute-start(f32[5,32,1,512]{3,1,2,0:T(8,128)S(1)} %copy.66), channel_id=1, source_target_pairs={{0,1},{1,2},{2,3},{4,5},{5,6},{6,7},{8,9},{9,10},{10,11},{12,13},{... | collective-permute-start | bytes 983048 | tf_op jit(solution)/shard_map/ppermute | solution.py:18
  17.5 1.3 copy-start.4
  17.5 1.3 copy-start.5
  28.9 3.6 %copy-start = (bf16[1,256,5,512]{3,1,2,0:T(8,128)(2,1)S(1)}, bf16[1,256,5,512]{3,1,2,0:T(8,128)(2,1)}, u32[]{:S(2)}) copy-start(bf16[1,256,5,512]{3,1,2,0:T(8,128)(2,1)} %param.15) | copy-start | bytes 3932164
  28.9 3.6 %copy-start.1 = (bf16[1,256,5,512]{3,1,2,0:T(8,128)(2,1)S(1)}, bf16[1,256,5,512]{3,1,2,0:T(8,128)(2,1)}, u32[]{:S(2)}) copy-start(bf16[1,256,5,512]{3,1,2,0:T(8,128)(2,1)} %param.16) | copy-start | bytes 3932164
  164.6 2.0 %copy-start.3 = (f32[5,32,4,512]{3,2,1,0:T(4,128)S(1)}, f32[5,32,4,512]{3,2,1,0:T(4,128)}, u32[]{:S(2)}) copy-start(f32[5,32,4,512]{3,2,1,0:T(4,128)} %param.9) | copy-start | bytes 3932164

commit v8 on v7

--- a/solution.py
+++ b/solution.py
@@ -121,8 +121,10 @@
     own_sol = pltpu.make_async_copy(solved.at[window(me)], out_ref.at[window(me)], local_sems.at[4])
 
     def order(step):
-        half = step // 2
-        return lax.select(step % 2 == 0, half, groups - 1 - half)
+        quarter, kind = step // 4, step % 4
+        near = lax.select(kind == 0, quarter, groups - 1 - quarter)
+        far = lax.select(kind == 2, groups // 4 + quarter, 3 * groups // 4 - 1 - quarter)
+        return lax.select(kind < 2, near, far)
 
     def send(i, carry):
         target = group * lax.rem(mine - order(i // group) + groups, groups) + i % group

time: 171 us -> 171 us (level)
  no operation moved by 1% of the time
where the time goes in v8:
time: 171 us; the launch traced here: 170 us
  Pallas kernels  130 us (76%)
  local copies, waits for them, and re-layouts  19.2 us (11%)
  other arithmetic  11.5 us (7%)
  starting transfers between devices  7.24 us (4%)
    pallas_call x1, Pallas kernels, owner_solve(): pl.pallas_call(functools.partial(owner_kernel, peers, group), out_shape=j...  130 us
    ppermute x2, starting transfers between devices, extended(): lax.ppermute(lax.slice_in_dim(block, block.shape[dim] - width, None, axis...  5.86 us
    transpose x1, other arithmetic, per_device(): residual.transpose(1, 2, 0, 3).reshape(line_count, fields * points)  5 us
    gather x2, local copies, waits for them, and re-layouts, per_device(): correction = jnp.take(returned, slot_ids, axis=0)  4.06 us
    select_n x2, other arithmetic, per_device(): outgoing = jnp.take(padded_rhs, line_of_slot, axis=0)  3.64 us
  transfers between devices with their start and end apart: 4, of which 1 were waited for; matrix products, arithmetic and copies ran while one was open for 4% of the time, Pallas kernels for 0%

profile of v8, /device:TPU:25, one launch (start us, length us, event | category | flops | bytes accessed | tf_op | source)
XLA Modules:
  0.0 169.7 jit_solution(9600135941832861041)
XLA Ops:
  0.0 0.8 fusion.6
  0.8 1.9 %collective-permute-start.1 = (f32[5,1,4,512]{3,2,1,0:T(4,128)S(1)}, f32[5,1,4,512]{3,2,1,0:T(4,128)S(1)}, u32[]{:S(2)}, u32[]{:S(2)}) collective-permute-start(f32[5,1,4,512]{3,2,1,0:T(4,128)S(1)} %get-tuple-element.45), channel_id=1, source_target_pairs={{0,4},{4,8},{8,12},{12,16},{16,20},{20,24},{24,28},{28,32},{32,36}... | collective-permute-start | bytes 122888 | tf_op jit(solution)/shard_map/ppermute | solution.py:18
  2.7 0.1 collective-permute-start
  2.8 2.5 %fusion.7 = (f32[5,32,1,512]{3,2,1,0:T(1,128)S(1)}, f32[5,32,1,512]{3,2,1,0:T(1,128)S(1)}) fusion(f32[5,32,4,512]{3,2,1,0:T(4,128)} %param.9), kind=kLoop, calls=%fused_computation.70 | loop fusion | bytes 1310720 | tf_op jit(solution)/shard_map/slice | solution.py:21
  5.3 1.3 collective-permute-start.2
  6.6 4.0 %collective-permute-start.3 = (f32[5,32,1,512]{3,1,2,0:T(8,128)S(1)}, f32[5,32,1,512]{3,1,2,0:T(8,128)S(1)}, u32[]{:S(2)}, u32[]{:S(2)}) collective-permute-start(f32[5,32,1,512]{3,1,2,0:T(8,128)S(1)} %copy.66), channel_id=1, source_target_pairs={{0,1},{1,2},{2,3},{4,5},{5,6},{6,7},{8,9},{9,10},{10,11},{12,13},{... | collective-permute-start | bytes 983048 | tf_op jit(solution)/shard_map/ppermute | solution.py:18
  10.6 0.0 copy-done.6
  10.6 0.4 slice_reduce_fusion.19
  11.0 0.2 slice_reduce_fusion.1
  11.2 0.0 copy-done.7
  11.2 0.1 copy.49
  11.3 0.1 copy.51
  11.4 0.1 mul.373
  11.5 0.1 reshape.87
  11.6 0.2 convert_reduce_fusion
  11.8 1.2 scatter_custom_fusion
  13.0 0.1 reduce_sum.14
  13.1 0.0 copy-done.8
  13.1 0.1 copy.52
  13.2 0.1 iota_compare_fusion
  13.3 0.1 copy.50
  13.4 0.0 collective-permute-done.1
  13.4 0.0 copy-done.2
  13.4 0.6 constant_dynamic-update-slice_fusion.1
  14.1 0.0 collective-permute-done
  14.1 0.2 slice_bitcast_fusion.9
  14.3 0.2 slice_bitcast_fusion.4
  14.6 1.4 collective-permute-done.2
  16.0 0.3 copy.54
  16.3 0.8 maximum_bitcast_fusion.7
  17.1 0.0 collective-permute-done.3
  17.1 0.3 copy.56
  17.5 0.0 copy-start.4
  17.5 0.0 copy-start.5
  17.5 0.6 maximum_bitcast_fusion.3
  18.1 0.7 copy-done.4
  18.8 0.0 copy-done.5
  18.8 5.0 %select_bitcast_fusion = f32[32,4,5,512]{3,1,0,2:T(4,128)S(1)} fusion(f32[5,32,4,512]{3,2,1,0:T(4,128)S(1)} %copy-done.4, f32[5,32,4,512]{3,2,1,0:T(4,128)S(1)} %copy-done.2, f32[32,4,512]{2,1,0:T(4,128)S(1)} %get-tuple-element.32, f32[5]{0:T(128)S(1)} %get-tuple-element.23, f32[32,4,512]{2,1,0:T(4,128)S(1)} %get-tuple-element.33, ...), kind=kLoop, calls=%fused_computation.6 | loop fusion | flops 14090240 | bytes 9503120 | tf_op jit(solution)/shard_map/transpose | solution.py:239
  23.8 0.8 copy.57
  24.6 1.0 copy.61
  25.7 0.1 concatenate.21
  25.8 3.1 %gather_fusion = f32[256,2560]{1,0:T(8,128)} fusion(f32[129,2560]{1,0:T(8,128)S(1)} %concatenate.21, s32[1024]{0:T(1024)S(1)} %get-tuple-element.51), kind=kCustom, calls=%fused_computation | custom fusion | bytes 5243904 | tf_op jit(solution)/shard_map/jit(_take)/gather | solution.py:250
  28.9 3.6 %broadcast_select_fusion.rhs_ref = f32[256,2560]{1,0:T(8,128)} fusion(f32[256,2560]{1,0:T(8,128)} %gather_fusion, pred[256]{0:T(512)(128)(4,1)S(1)} %compare_and_fusion), kind=kLoop, calls=%fused_computation.5 | loop fusion | flops 655360 | bytes 5243136 | tf_op jit(solution)/shard_map/jit(_take)/select_n | solution.py:250
  32.5 130.0 %shard_map.91 = f32[256,2560]{1,0:T(8,128)S(1)} custom-call(f32[256,2560]{1,0:T(8,128)} %broadcast_select_fusion.rhs_ref, bf16[5,256,512]{2,1,0:T(8,128)(2,1)S(1)} %bitcast.71, bf16[5,256,512]{2,1,0:T(8,128)(2,1)S(1)} %bitcast.72, bf16[25,256,512]{2,1,0:T(8,128)(2,1)} %bitcast.74), custom_call_target="tpu_custom_call" | custom-call | tf_op jit(solution)/shard_map/pallas_call | solution.py:192
  162.5 2.1 %gather_fusion.1 = f32[128,2560]{1,0:T(8,128)} fusion(f32[256,2560]{1,0:T(8,128)S(1)} %shard_map.91, s32[1024]{0:T(1024)S(1)} %get-tuple-element.50), kind=kCustom, calls=%fused_computation.1 | custom fusion | bytes 2621952 | tf_op jit(solution)/shard_map/jit(_take)/gather | solution.py:258
  164.6 2.0 %gather.12 = f32[32,4,5,512]{3,2,1,0:T(8,128)S(1)} reshape(f32[128,2560]{1,0:T(8,128)} %gather_fusion.1) | data formatting | bytes 2621440 | tf_op jit(solution)/shard_map/jit(_take)/gather | solution.py:258
  166.6 1.2 bitcast_add_fusion
  167.8 1.9 %copy.60 = f32[5,32,4,512]{3,2,1,0:T(4,128)} copy(f32[5,32,4,512]{3,1,2,0:T(8,128)S(1)} %bitcast_add_fusion) | data formatting | bytes 2621440 | tf_op jit(solution)/shard_map/add | solution.py:260
  (21 shorter events, 0.1 us)
Async XLA Ops:
  0.8 12.6 %collective-permute-start.1 = (f32[5,1,4,512]{3,2,1,0:T(4,128)S(1)}, f32[5,1,4,512]{3,2,1,0:T(4,128)S(1)}, u32[]{:S(2)}, u32[]{:S(2)}) collective-permute-start(f32[5,1,4,512]{3,2,1,0:T(4,128)S(1)} %get-tuple-element.45), channel_id=1, source_target_pairs={{0,4},{4,8},{8,12},{12,16},{16,20},{20,24},{24,28},{28,32},{32,36}... | collective-permute-start | bytes 122888 | tf_op jit(solution)/shard_map/ppermute | solution.py:18
  2.7 8.0 %copy-start.6 = (f32[4,5,5]{2,0,1:T(4,128)S(1)}, f32[4,5,5]{2,0,1:T(4,128)}, u32[]{:S(2)}) copy-start(f32[4,5,5]{2,0,1:T(4,128)} %param.14) | copy-start | bytes 1204
  2.7 8.5 %copy-start.7 = (s32[1,32,4,1]{1,3,2,0:T(1,128)S(1)}, s32[1,32,4,1]{1,3,2,0:T(1,128)}, u32[]{:S(2)}) copy-start(s32[1,32,4,1]{1,3,2,0:T(1,128)} %param.13) | copy-start | bytes 1540
  2.7 10.4 %copy-start.8 = (s32[32,4]{0,1:T(4,128)S(1)}, s32[32,4]{0,1:T(4,128)}, u32[]{:S(2)}) copy-start(s32[32,4]{0,1:T(4,128)} %param.12) | copy-start | bytes 1540
  2.7 10.8 %copy-start.2 = (f32[5,32,4,512]{3,2,1,0:T(4,128)S(1)}, f32[5,32,4,512]{3,2,1,0:T(4,128)}, u32[]{:S(2)}) copy-start(f32[5,32,4,512]{3,2,1,0:T(4,128)} %param.9) | copy-start | bytes 3932164
  2.7 11.4 %collective-permute-start = (f32[5,1,4,512]{3,2,1,0:T(4,128)S(1)}, f32[5,1,4,512]{3,2,1,0:T(4,128)S(1)}, u32[]{:S(2)}, u32[]{:S(2)}) collective-permute-start(f32[5,1,4,512]{3,2,1,0:T(4,128)S(1)} %get-tuple-element.44), channel_id=1, source_target_pairs={{4,0},{8,4},{12,8},{16,12},{20,16},{24,20},{28,24},{32,28},{36,32}... | collective-permute-start | bytes 122888 | tf_op jit(solution)/shard_map/ppermute | solution.py:21
  5.3 10.7 %collective-permute-start.2 = (f32[5,32,1,512]{3,1,2,0:T(8,128)S(1)}, f32[5,32,1,512]{3,1,2,0:T(8,128)S(1)}, u32[]{:S(2)}, u32[]{:S(2)}) collective-permute-start(f32[5,32,1,512]{3,1,2,0:T(8,128)S(1)} %copy.67), channel_id=1, source_target_pairs={{1,0},{2,1},{3,2},{5,4},{6,5},{7,6},{9,8},{10,9},{11,10},{13,12},{... | collective-permute-start | bytes 983048 | tf_op jit(solution)/shard_map/ppermute | solution.py:21
  6.6 10.5 %collective-permute-start.3 = (f32[5,32,1,512]{3,1,2,0:T(8,128)S(1)}, f32[5,32,1,512]{3,1,2,0:T(8,128)S(1)}, u32[]{:S(2)}, u32[]{:S(2)}) collective-permute-start(f32[5,32,1,512]{3,1,2,0:T(8,128)S(1)} %copy.66), channel_id=1, source_target_pairs={{0,1},{1,2},{2,3},{4,5},{5,6},{6,7},{8,9},{9,10},{10,11},{12,13},{... | collective-permute-start | bytes 983048 | tf_op jit(solution)/shard_map/ppermute | solution.py:18
  17.5 1.3 copy-start.4
  17.5 1.3 copy-start.5
  28.9 3.6 %copy-start = (bf16[1,256,5,512]{3,1,2,0:T(8,128)(2,1)S(1)}, bf16[1,256,5,512]{3,1,2,0:T(8,128)(2,1)}, u32[]{:S(2)}) copy-start(bf16[1,256,5,512]{3,1,2,0:T(8,128)(2,1)} %param.15) | copy-start | bytes 3932164
  28.9 3.6 %copy-start.1 = (bf16[1,256,5,512]{3,1,2,0:T(8,128)(2,1)S(1)}, bf16[1,256,5,512]{3,1,2,0:T(8,128)(2,1)}, u32[]{:S(2)}) copy-start(bf16[1,256,5,512]{3,1,2,0:T(8,128)(2,1)} %param.16) | copy-start | bytes 3932164
  164.6 2.0 %copy-start.3 = (f32[5,32,4,512]{3,2,1,0:T(4,128)S(1)}, f32[5,32,4,512]{3,2,1,0:T(4,128)}, u32[]{:S(2)}) copy-start(f32[5,32,4,512]{3,2,1,0:T(4,128)} %param.9) | copy-start | bytes 3932164

commit v9 on v8

--- a/solution.py
+++ b/solution.py
@@ -247,7 +247,7 @@
     padded_rhs = jnp.concatenate(
         [line_rhs, jnp.full((1, fields * points), jnp.nan, jnp.float32)], axis=0
     )
-    outgoing = jnp.take(padded_rhs, line_of_slot, axis=0)
+    outgoing = jnp.take(padded_rhs, line_of_slot, axis=0, mode="clip")
     returned = owner_solve(
         outgoing,
         lower_coef[0].transpose(1, 0, 2),
@@ -255,7 +255,7 @@
         pivot_inverse[0].transpose(1, 0, 2),
         circ_devices,
     )
-    correction = jnp.take(returned, slot_ids, axis=0)
+    correction = jnp.take(returned, slot_ids, axis=0, mode="clip")
     correction = correction.reshape(circ_cells, axial_cells, fields, points).transpose(2, 0, 1, 3)
     return adjoint + correction
 

time: 171 us -> 170 us (level)
  other arithmetic: 11.5 us -> 7.8 us
  local copies, waits for them, and re-layouts: 19.2 us -> 21.6 us
    select_n x3 -> x0, other arithmetic: 3.64 us -> none  [the longest x2 3.64 us: per_device(): outgoing = jnp.take(padded_rhs, line_of_slot, axis=0)]
    unnamed x25, local copies, waits for them, and re-layouts: 2.62 us -> 5.25 us
    gather x3 -> x2, local copies, waits for them, and re-layouts: 7.11 us -> 5.15 us  [the longest x1 3.05 us: per_device(): outgoing = jnp.take(padded_rhs, line_of_slot, axis=0, mode='clip')]
    reshape x1, local copies, waits for them, and re-layouts: 0.1 us -> 1.97 us  [per_device(): correction.reshape(circ_cells, axial_cells, fields, points)]
where the time goes in v9:
time: 170 us; the launch traced here: 169 us
  Pallas kernels  130 us (76%)
  local copies, waits for them, and re-layouts  21.6 us (13%)
  other arithmetic  7.8 us (5%)
  starting transfers between devices  7.24 us (4%)
    pallas_call x1, Pallas kernels, owner_solve(): pl.pallas_call(functools.partial(owner_kernel, peers, group), out_shape=j...  130 us
    ppermute x2, starting transfers between devices, extended(): lax.ppermute(lax.slice_in_dim(block, block.shape[dim] - width, None, axis...  5.86 us
    unnamed x25, local copies, waits for them, and re-layouts  5.25 us
    transpose x1, other arithmetic, per_device(): residual.transpose(1, 2, 0, 3).reshape(line_count, fields * points)  5 us
  transfers between devices with their start and end apart: 4, of which 1 were waited for; matrix products, arithmetic and copies ran while one was open for 4% of the time, Pallas kernels for 0%

profile of v9, /device:TPU:25, one launch (start us, length us, event | category | flops | bytes accessed | tf_op | source)
XLA Modules:
  0.0 168.6 jit_solution(11293815213000025330)
XLA Ops:
  0.0 0.8 fusion.7
  0.8 1.9 %collective-permute-start.1 = (f32[5,1,4,512]{3,2,1,0:T(4,128)S(1)}, f32[5,1,4,512]{3,2,1,0:T(4,128)S(1)}, u32[]{:S(2)}, u32[]{:S(2)}) collective-permute-start(f32[5,1,4,512]{3,2,1,0:T(4,128)S(1)} %get-tuple-element.45), channel_id=1, source_target_pairs={{0,4},{4,8},{8,12},{12,16},{16,20},{20,24},{24,28},{28,32},{32,36}... | collective-permute-start | bytes 122888 | tf_op jit(solution)/shard_map/ppermute | solution.py:18
  2.7 0.1 collective-permute-start
  2.8 2.5 %fusion.8 = (f32[5,32,1,512]{3,2,1,0:T(1,128)S(1)}, f32[5,32,1,512]{3,2,1,0:T(1,128)S(1)}) fusion(f32[5,32,4,512]{3,2,1,0:T(4,128)} %param.9), kind=kLoop, calls=%fused_computation.65 | loop fusion | bytes 1310720 | tf_op jit(solution)/shard_map/slice | solution.py:21
  5.3 1.3 collective-permute-start.2
  6.6 4.0 %collective-permute-start.3 = (f32[5,32,1,512]{3,1,2,0:T(8,128)S(1)}, f32[5,32,1,512]{3,1,2,0:T(8,128)S(1)}, u32[]{:S(2)}, u32[]{:S(2)}) collective-permute-start(f32[5,32,1,512]{3,1,2,0:T(8,128)S(1)} %copy.55), channel_id=1, source_target_pairs={{0,1},{1,2},{2,3},{4,5},{5,6},{6,7},{8,9},{9,10},{10,11},{12,13},{... | collective-permute-start | bytes 983048 | tf_op jit(solution)/shard_map/ppermute | solution.py:18
  10.6 0.0 copy-done.6
  10.6 0.4 slice_reduce_fusion.19
  11.0 0.2 slice_reduce_fusion.1
  11.2 0.0 copy-done.7
  11.2 0.1 copy.48
  11.3 0.0 copy-done.8
  11.3 0.1 copy.41
  11.4 0.1 iota_compare_fusion
  11.5 0.1 copy.47
  11.6 0.1 mul.472
  11.7 0.1 eq.15
  11.8 0.2 convert_reduce_fusion
  12.0 1.2 scatter_custom_fusion
  13.2 0.0 collective-permute-done.1
  13.2 0.0 copy-done.2
  13.2 0.6 constant_dynamic-update-slice_fusion.1
  13.8 0.0 collective-permute-done
  13.9 0.2 slice_bitcast_fusion.9
  14.1 0.2 slice_bitcast_fusion.4
  14.4 1.6 collective-permute-done.2
  16.0 0.3 copy.43
  16.3 0.8 maximum_bitcast_fusion.7
  17.1 0.0 collective-permute-done.3
  17.1 0.3 copy.45
  17.5 0.0 copy-start.4
  17.5 0.0 copy-start.5
  17.5 0.6 maximum_bitcast_fusion.3
  18.1 0.7 copy-done.4
  18.8 0.0 copy-done.5
  18.8 5.0 %select_bitcast_fusion = f32[32,4,5,512]{3,1,0,2:T(4,128)S(1)} fusion(f32[5,32,4,512]{3,2,1,0:T(4,128)S(1)} %copy-done.4, f32[5,32,4,512]{3,2,1,0:T(4,128)S(1)} %copy-done.2, f32[32,4,512]{2,1,0:T(4,128)S(1)} %get-tuple-element.32, f32[5]{0:T(128)S(1)} %get-tuple-element.23, f32[32,4,512]{2,1,0:T(4,128)S(1)} %get-tuple-element.33, ...), kind=kLoop, calls=%fused_computation.4 | loop fusion | flops 14090240 | bytes 9503120 | tf_op jit(solution)/shard_map/transpose | solution.py:239
  23.8 0.8 copy.46
  24.6 1.0 copy.52
  25.7 0.1 concatenate.21
  25.8 3.1 %gather_fusion = f32[256,2560]{1,0:T(8,128)} fusion(f32[129,2560]{1,0:T(8,128)S(1)} %concatenate.21, s32[1024]{0:T(1024)S(1)} %get-tuple-element.53), kind=kCustom, calls=%fused_computation | custom fusion | bytes 5243904 | tf_op jit(solution)/shard_map/jit(_take)/gather | solution.py:250
  28.9 1.3 copy-done
  30.2 1.3 copy-done.1
  31.5 130.0 %shard_map.91 = f32[256,2560]{1,0:T(8,128)S(1)} custom-call(f32[256,2560]{1,0:T(8,128)} %gather_fusion, bf16[5,256,512]{2,1,0:T(8,128)(2,1)S(1)} %bitcast.74, bf16[5,256,512]{2,1,0:T(8,128)(2,1)S(1)} %bitcast.75, bf16[25,256,512]{2,1,0:T(8,128)(2,1)} %bitcast.77), custom_call_target="tpu_custom_call" | custom-call | tf_op jit(solution)/shard_map/pallas_call | solution.py:192
  161.5 2.1 %gather_fusion.1 = f32[128,2560]{1,0:T(8,128)} fusion(f32[256,2560]{1,0:T(8,128)S(1)} %shard_map.91, s32[1024]{0:T(1024)S(1)} %get-tuple-element.52), kind=kCustom, calls=%fused_computation.1 | custom fusion | bytes 2621952 | tf_op jit(solution)/shard_map/jit(_take)/gather | solution.py:258
  163.6 2.0 %reshape.75 = f32[32,4,5,512]{3,2,1,0:T(8,128)S(1)} reshape(f32[128,2560]{1,0:T(8,128)} %gather_fusion.1) | data formatting | bytes 2621440 | tf_op jit(solution)/shard_map/reshape | solution.py:259
  165.6 0.0 copy-done.3
  165.6 1.1 bitcast_add_fusion
  166.7 1.9 %copy.51 = f32[5,32,4,512]{3,2,1,0:T(4,128)} copy(f32[5,32,4,512]{3,1,2,0:T(8,128)S(1)} %bitcast_add_fusion) | data formatting | bytes 2621440 | tf_op jit(solution)/shard_map/add | solution.py:260
  (15 shorter events, 0.1 us)
Async XLA Ops:
  0.8 12.4 %collective-permute-start.1 = (f32[5,1,4,512]{3,2,1,0:T(4,128)S(1)}, f32[5,1,4,512]{3,2,1,0:T(4,128)S(1)}, u32[]{:S(2)}, u32[]{:S(2)}) collective-permute-start(f32[5,1,4,512]{3,2,1,0:T(4,128)S(1)} %get-tuple-element.45), channel_id=1, source_target_pairs={{0,4},{4,8},{8,12},{12,16},{16,20},{20,24},{24,28},{28,32},{32,36}... | collective-permute-start | bytes 122888 | tf_op jit(solution)/shard_map/ppermute | solution.py:18
  2.7 8.0 %copy-start.6 = (f32[4,5,5]{2,0,1:T(4,128)S(1)}, f32[4,5,5]{2,0,1:T(4,128)}, u32[]{:S(2)}) copy-start(f32[4,5,5]{2,0,1:T(4,128)} %param.14) | copy-start | bytes 1204
  2.7 8.5 %copy-start.7 = (s32[1,32,4,1]{1,3,2,0:T(1,128)S(1)}, s32[1,32,4,1]{1,3,2,0:T(1,128)}, u32[]{:S(2)}) copy-start(s32[1,32,4,1]{1,3,2,0:T(1,128)} %param.13) | copy-start | bytes 1540
  2.7 8.6 %copy-start.8 = (s32[32,4]{0,1:T(4,128)S(1)}, s32[32,4]{0,1:T(4,128)}, u32[]{:S(2)}) copy-start(s32[32,4]{0,1:T(4,128)} %param.12) | copy-start | bytes 1540
  2.7 10.6 %copy-start.2 = (f32[5,32,4,512]{3,2,1,0:T(4,128)S(1)}, f32[5,32,4,512]{3,2,1,0:T(4,128)}, u32[]{:S(2)}) copy-start(f32[5,32,4,512]{3,2,1,0:T(4,128)} %param.9) | copy-start | bytes 3932164
  2.7 11.2 %collective-permute-start = (f32[5,1,4,512]{3,2,1,0:T(4,128)S(1)}, f32[5,1,4,512]{3,2,1,0:T(4,128)S(1)}, u32[]{:S(2)}, u32[]{:S(2)}) collective-permute-start(f32[5,1,4,512]{3,2,1,0:T(4,128)S(1)} %get-tuple-element.44), channel_id=1, source_target_pairs={{4,0},{8,4},{12,8},{16,12},{20,16},{24,20},{28,24},{32,28},{36,32}... | collective-permute-start | bytes 122888 | tf_op jit(solution)/shard_map/ppermute | solution.py:21
  5.3 10.7 %collective-permute-start.2 = (f32[5,32,1,512]{3,1,2,0:T(8,128)S(1)}, f32[5,32,1,512]{3,1,2,0:T(8,128)S(1)}, u32[]{:S(2)}, u32[]{:S(2)}) collective-permute-start(f32[5,32,1,512]{3,1,2,0:T(8,128)S(1)} %copy.56), channel_id=1, source_target_pairs={{1,0},{2,1},{3,2},{5,4},{6,5},{7,6},{9,8},{10,9},{11,10},{13,12},{... | collective-permute-start | bytes 983048 | tf_op jit(solution)/shard_map/ppermute | solution.py:21
  6.6 10.5 %collective-permute-start.3 = (f32[5,32,1,512]{3,1,2,0:T(8,128)S(1)}, f32[5,32,1,512]{3,1,2,0:T(8,128)S(1)}, u32[]{:S(2)}, u32[]{:S(2)}) collective-permute-start(f32[5,32,1,512]{3,1,2,0:T(8,128)S(1)} %copy.55), channel_id=1, source_target_pairs={{0,1},{1,2},{2,3},{4,5},{5,6},{6,7},{8,9},{9,10},{10,11},{12,13},{... | collective-permute-start | bytes 983048 | tf_op jit(solution)/shard_map/ppermute | solution.py:18
  17.5 1.3 copy-start.4
  17.5 1.3 copy-start.5
  28.9 1.3 copy-start
  30.2 1.3 copy-start.1
  163.6 2.0 %copy-start.3 = (f32[5,32,4,512]{3,2,1,0:T(4,128)S(1)}, f32[5,32,4,512]{3,2,1,0:T(4,128)}, u32[]{:S(2)}) copy-start(f32[5,32,4,512]{3,2,1,0:T(4,128)} %param.9) | copy-start | bytes 3932164
